TPU v7x, 256 devices: a whole 4x4x8 slice. The times are simulated.
256 devices in a mesh: row: 32 (over z, y), col: 8 (over x, core).
Axes of the slice: x: 4, y: 4, z: 8, core: 2. Of those that a mesh axis runs over, the one named last changes fastest.
Arguments:
- feats: bfloat16 [131072, 256], P(('row', 'col')), may hold values from -6 to 6
- w_msg: bfloat16 [256, 256], replicated, may hold values from -0.375 to 0.375
- w_self: bfloat16 [256, 256], replicated, may hold values from -0.375 to 0.375
- bias: float32 [256], replicated, may hold values from -3 to 3
- hit_mask: int32 [131072], P(('row', 'col')), may hold values 0 or 1
- block_cols: int32 [32, 8, 96], P('row', 'col'), may hold values from 0 to 127, as said below
- block_count: int32 [32, 8], P('row', 'col'), may hold values from 32 to 96, as said below
- edge_vals: bfloat16 [32, 8, 96, 128, 128], P('row', 'col'), may hold values from -0.125 to 0.125
- grad_out: bfloat16 [131072, 256], P(('row', 'col')), may hold values from -3 to 3
Outputs:
- hidden: bfloat16 [131072, 256], P(('row', 'col'))
- grad_feats: bfloat16 [131072, 256], P(('row', 'col'))
- edge_grad: bfloat16 [32, 8, 96, 128, 128], P('row', 'col')
- w_msg_grad: float32 [256, 256], replicated
- w_self_grad: float32 [256, 256], replicated
- bias_grad: float32 [256], replicated
Inputs may be any that keep to these rules, and one draw needn't show every extreme that they name: `block_cols`: slot s of a tile serves the tile's local block row s % 32; the block columns of the slots that serve one block row of one tile are different. Slots from block_count on are unused.
All inputs are finite; a program needn't handle non-finite values. No bound on the sum of `hit_mask` on one device may be relied on, other than what follows from the above.
Results may differ from a plain program's by a relative error of at most 0.015.
Values may be sent and summed in bfloat16 or wider, within the bound.
A program may use at most 128 MiB of HBM per device.

v0:
```python
import math

import jax
import jax.numpy as jnp
from jax import lax
from jax.sharding import PartitionSpec as P


def activate(pre, row_mask, grad_in):
    sig = jax.nn.sigmoid(pre)
    hidden = (pre * sig * row_mask).astype(jnp.bfloat16)
    deriv = sig * (1.0 + pre * (1.0 - sig))
    grad_pre = (grad_in.astype(jnp.float32) * row_mask * deriv).astype(jnp.bfloat16)
    return (hidden, grad_pre)


def per_device(feats, w_msg, w_self, bias, hit_mask, block_cols, block_count, edge_vals, grad_out):
    row_count = lax.axis_size("row")
    col_count = lax.axis_size("col")
    own_rows = feats.shape[0]
    width = feats.shape[1]
    row_mask = hit_mask.astype(jnp.float32)[:, None]
    messages = (jnp.dot(feats, w_msg, preferred_element_type=jnp.float32) * row_mask).astype(
        jnp.bfloat16
    )
    column_msgs = lax.all_gather(messages, "row", axis=0, tiled=True)
    slot_cols = block_cols[0, 0]
    edge_block = edge_vals[0, 0]
    slot_total = edge_block.shape[0]
    edge_size = edge_block.shape[1]
    tile_rows = col_count * own_rows // edge_size
    tile_cols = row_count * own_rows // edge_size
    slot_depth = slot_total // tile_rows
    slot_flags = jnp.arange(slot_total, dtype=jnp.int32) < block_count[0, 0]
    edge_live = (edge_block * slot_flags.astype(jnp.bfloat16)[:, None, None]).reshape(
        slot_depth, tile_rows, edge_size, edge_size
    )
    col_blocks = column_msgs.reshape(tile_cols, edge_size, width)[slot_cols].reshape(
        slot_depth, tile_rows, edge_size, width
    )
    partial_value = jnp.einsum(
        "krij,krjf->rif", edge_live, col_blocks, preferred_element_type=jnp.float32
    ).reshape(tile_rows * edge_size, width)
    summed = lax.psum_scatter(
        partial_value.astype(jnp.bfloat16), "col", scatter_dimension=0, tiled=True
    ).astype(jnp.float32)
    pre = summed + jnp.dot(feats, w_self, preferred_element_type=jnp.float32) + bias
    hidden, grad_pre = activate(pre, row_mask, grad_out)
    grad_rows_all = lax.all_gather(grad_pre, "col", axis=0, tiled=True)
    grad_tile = grad_rows_all.reshape(tile_rows, edge_size, width)
    backward = jnp.einsum(
        "krij,rif->krjf", edge_live, grad_tile, preferred_element_type=jnp.float32
    ).reshape(slot_total, edge_size, width)
    back_part = jax.ops.segment_sum(backward, slot_cols, num_segments=tile_cols).reshape(
        tile_cols * edge_size, width
    )
    edge_grad = (
        jnp.einsum(
            "rif,krjf->krij", grad_tile, col_blocks, preferred_element_type=jnp.float32
        ).reshape(slot_total, edge_size, edge_size)
        * slot_flags.astype(jnp.float32)[:, None, None]
    ).astype(jnp.bfloat16)
    grad_sum = lax.psum_scatter(
        back_part.astype(jnp.bfloat16), "row", scatter_dimension=0, tiled=True
    ).astype(jnp.float32)
    grad_msg = (grad_sum * row_mask).astype(jnp.bfloat16)
    grad_feats = (
        jnp.einsum("hg,fg->hf", grad_msg, w_msg, preferred_element_type=jnp.float32)
        + jnp.einsum("hg,fg->hf", grad_pre, w_self, preferred_element_type=jnp.float32)
    ).astype(jnp.bfloat16)
    local_msg = jnp.einsum("hf,hg->fg", feats, grad_msg, preferred_element_type=jnp.float32)
    local_self = jnp.einsum("hf,hg->fg", feats, grad_pre, preferred_element_type=jnp.float32)
    local_bias = jnp.sum(grad_pre.astype(jnp.float32), axis=0)
    total_msg, total_self, total_bias = lax.psum(
        (local_msg, local_self, local_bias), ("row", "col")
    )
    factor = 1.0 / math.sqrt(own_rows * row_count * col_count)
    return (
        hidden,
        grad_feats,
        edge_grad[None, None],
        total_msg * factor,
        total_self * factor,
        total_bias * factor,
    )


def solution(mesh):
    placed = (
        P(("row", "col"), None),
        P(),
        P(),
        P(),
        P(("row", "col")),
        P("row", "col", None),
        P("row", "col"),
        P("row", "col", None, None, None),
        P(("row", "col"), None),
    )
    return jax.shard_map(
        per_device,
        mesh=mesh,
        in_specs=placed,
        out_specs=(
            P(("row", "col"), None),
            P(("row", "col"), None),
            P("row", "col", None, None, None),
            P(),
            P(),
            P(),
        ),
        check_vma=False,
    )
```

profile of v0, /device:TPU:1, one launch (start us, length us, event | category | flops | bytes accessed | tf_op | source)
XLA Modules:
  0.0 757.5 jit_solution(17679265204071514697)
XLA Ops:
  7.2 0.0 copy-start
  7.2 0.0 all-gather.3.cloned.1.call-start
  7.2 0.7 convert_element_type.67
  7.9 0.2 copy-done
  8.1 1.8 fusion.12
  10.0 0.0 all-gather.3.cloned.1.call-update
  10.0 0.0 reduce-scatter.3.cloned.1.call-start
  10.7 0.7 fusion.16
  11.4 100.8 %all-gather.3.cloned.1.call-done = bf16[16384,256]{1,0:T(8,128)(2,1)} async-done(((bf16[512,256]{1,0:T(8,128)(2,1)}), bf16[16384,256]{1,0:T(8,128)(2,1)}) %all-gather.3.cloned.1.call-update) | async-done | bytes 8388624 | tf_op jit(solution)/shard_map/all_gather | solution.py:26
  112.1 0.0 copy-start.2
  112.1 9.5 %gather_fusion = bf16[96,128,256]{2,1,0:T(8,128)(2,1)} fusion(bf16[128,128,256]{2,1,0:T(8,128)(2,1)} %bitcast.53, s32[1024]{0:T(1024)S(1)} %pad_clamp_fusion), kind=kCustom, calls=%fused_computation | custom fusion | bytes 12583296 | tf_op jit(solution)/shard_map/gather | solution.py:38
  121.6 0.0 copy-done.2
  121.6 0.0 copy-start.5
  121.6 5.5 bitcast_convert_fusion
  127.1 0.0 reduce-scatter.3.cloned.1.call-update
  127.1 0.0 all-gather.5.cloned.1.call-start
  127.2 31.9 %reduce-scatter.3.cloned.1.call-done = bf16[512,256]{1,0:T(8,128)(2,1)} async-done(((bf16[4096,256]{1,0:T(8,128)(2,1)}), bf16[512,256]{1,0:T(8,128)(2,1)}) %reduce-scatter.3.cloned.1.call-update) | async-done | bytes 262160 | tf_op jit(solution)/shard_map/reduce_scatter | solution.py:44
  159.1 0.0 copy-done.5
  159.1 2.3 convert_reduce_fusion
  161.4 0.0 all-gather.5.cloned.1.call-update
  161.4 0.0 reduce-scatter.5.cloned.1.call-start
  161.5 29.5 %all-gather.5.cloned.1.call-done = bf16[4096,256]{1,0:T(8,128)(2,1)} async-done(((bf16[512,256]{1,0:T(8,128)(2,1)}), bf16[4096,256]{1,0:T(8,128)(2,1)}) %all-gather.5.cloned.1.call-update) | async-done | bytes 2097168 | tf_op jit(solution)/shard_map/all_gather | solution.py:49
  191.0 8.0 %convolution_bitcast_fusion = f32[3,32,128,256]{2,3,0,1:T(8,128)} fusion(bf16[32,128,256,1]{2,1,3,0:T(8,128)(2,1)} %bitcast.51, bf16[3,32,128,128]{3,2,1,0:T(8,128)(2,1)S(1)} %bitcast.55, bf16[3,32]{0,1:T(8,128)(2,1)S(1)} %fusion.15), kind=kOutput, calls=%fused_computation.7 | convolution fusion | flops 811597824 | bytes 17825984 | tf_op jit(solution)/shard_map/krij,rif->krjf/dot_general | solution.py:51
  199.0 12.6 %copy.22 = f32[3,32,128,256]{3,2,1,0:T(8,128)} copy(f32[3,32,128,256]{2,3,0,1:T(8,128)} %convolution_bitcast_fusion) | data formatting | bytes 25165824 | tf_op jit(solution)/shard_map/krij,rif->krjf/transpose | solution.py:51
  211.6 0.0 copy-start.6
  211.6 7.8 %broadcast_in_dim.2 = f32[128,128,256]{2,1,0:T(8,128)} broadcast(f32[]{:T(128)} %constant.4.clone.1), dimensions={} | broadcast | bytes 16777220 | tf_op jit(solution)/shard_map/broadcast_in_dim | solution.py:54
  219.4 0.0 copy-done.6
  219.4 28.8 %scatter_fusion = f32[128,128,256]{2,1,0:T(8,128)} fusion(f32[128,128,256]{2,1,0:T(8,128)} %broadcast_in_dim.2, s32[96]{0:T(128)S(1)} %bitcast.57, f32[96,128,256]{2,1,0:T(8,128)} %bitcast.46), kind=kCustom, calls=%fused_computation.1 | custom fusion | flops 3145728 | bytes 37749120 | tf_op jit(solution)/shard_map/scatter-add | solution.py:54
  248.2 9.0 %convert_element_type.75 = bf16[128,128,256]{2,1,0:T(8,128)(2,1)} convert(f32[128,128,256]{2,1,0:T(8,128)} %scatter_fusion) | non-fusion elementwise | flops 4194304 | bytes 25165824 | tf_op jit(solution)/shard_map/convert_element_type | solution.py:64
  257.2 0.0 copy-start.3
  257.2 0.0 copy-start.1
  257.2 0.0 reduce-scatter.5.cloned.1.call-update
  257.3 0.0 all-reduce.3.cloned.1.call-start
  257.3 77.5 %psum.23 = f32[256]{0:T(256)S(1)} all-reduce(f32[256]{0:T(256)S(1)} %get-tuple-element.20), channel_id=1, replica_groups=mesh['row'=32,'col'=8] {'row','col'}, use_global_device_ids=true, to_apply=%region_6.0 | all-reduce | flops 256 | bytes 2048 | tf_op jit(solution)/shard_map/psum | solution.py:74
  334.8 0.6 broadcast_multiply_fusion.2
  335.4 0.0 copy-done.3
  335.4 1.0 convolution_bitcast_fusion.1
  336.4 0.0 copy-done.1
  336.4 7.3 fusion.4
  343.7 6.6 copy.24
  350.3 0.0 copy-start.4
  350.3 5.1 multiply_convert_fusion
  355.4 130.0 %reduce-scatter.5.cloned.1.call-done = bf16[512,256]{1,0:T(8,128)(2,1)} async-done(((bf16[16384,256]{1,0:T(8,128)(2,1)}), bf16[512,256]{1,0:T(8,128)(2,1)}) %reduce-scatter.5.cloned.1.call-update) | async-done | bytes 262160 | tf_op jit(solution)/shard_map/reduce_scatter | solution.py:63
  485.4 2.0 convolution_bitcast_fusion.2
  487.4 0.0 all-reduce.3.cloned.1.call-update
  487.4 0.0 copy-done.4
  487.4 1.2 fusion.14
  488.7 1.0 fusion.13
  489.6 258.6 %all-reduce.3.cloned.1.call-done = (f32[256,256]{0,1:T(8,128)}, f32[256,256]{0,1:T(8,128)}) async-done(((f32[256,256]{0,1:T(8,128)}, f32[256,256]{0,1:T(8,128)}), (f32[256,256]{0,1:T(8,128)}, f32[256,256]{0,1:T(8,128)})) %all-reduce.3.cloned.1.call-update) | async-done | bytes 524304 | tf_op jit(solution)/shard_map/psum | solution.py:74
  748.2 1.1 broadcast_multiply_fusion
  749.3 0.8 copy.26
  750.1 0.8 copy.25
  (3 shorter events, 0.0 us)
Async XLA Ops:
  7.2 1.0 copy-start
  7.2 105.0 %all-gather.3.cloned.1.call-start = ((), (), s32[]{:S(2)}) async-start(), calls=%async_computation.2 | async-start | bytes 8650752 | tf_op jit(solution)/shard_map/all_gather | solution.py:26
  10.0 149.1 %reduce-scatter.3.cloned.1.call-start = ((), (), s32[]{:S(2)}) async-start(), calls=%async_computation.3 | async-start | bytes 2359296 | tf_op jit(solution)/shard_map/reduce_scatter | solution.py:44
  112.1 9.5 %copy-start.2 = (bf16[1,1,96,128,128]{4,3,2,1,0:T(8,128)(2,1)S(1)}, bf16[1,1,96,128,128]{4,3,2,1,0:T(8,128)(2,1)}, u32[]{:S(2)}) copy-start(bf16[1,1,96,128,128]{4,3,2,1,0:T(8,128)(2,1)} %param.16) | copy-start | bytes 9437188
  121.6 37.5 %copy-start.5 = (bf16[256,256]{1,0:T(8,128)(2,1)S(1)}, bf16[256,256]{1,0:T(8,128)(2,1)}, u32[]{:S(2)}) copy-start(bf16[256,256]{1,0:T(8,128)(2,1)} %param.11) | copy-start | bytes 393220
  127.1 63.9 %all-gather.5.cloned.1.call-start = ((), (), s32[]{:S(2)}) async-start(), calls=%async_computation.4 | async-start | bytes 2359296 | tf_op jit(solution)/shard_map/all_gather | solution.py:49
  161.4 324.0 %reduce-scatter.5.cloned.1.call-start = ((), (), s32[]{:S(2)}) async-start(), calls=%async_computation.5 | async-start | bytes 8650752 | tf_op jit(solution)/shard_map/reduce_scatter | solution.py:63
  211.6 7.9 %copy-start.6 = (s32[1,1,96]{2,1,0:T(1,128)S(1)}, s32[1,1,96]{2,1,0:T(1,128)}, u32[]{:S(2)}) copy-start(s32[1,1,96]{2,1,0:T(1,128)} %param.14) | copy-start | bytes 1156
  257.2 78.2 %copy-start.3 = (bf16[512,256]{1,0:T(8,128)(2,1)S(1)}, bf16[512,256]{1,0:T(8,128)(2,1)}, u32[]{:S(2)}) copy-start(bf16[512,256]{1,0:T(8,128)(2,1)} %get-tuple-element.21) | copy-start | bytes 786436
  257.2 79.1 %copy-start.1 = (bf16[4096,256]{1,0:T(8,128)(2,1)S(1)}, bf16[4096,256]{1,0:T(8,128)(2,1)}, u32[]{:S(2)}) copy-start(bf16[4096,256]{1,0:T(8,128)(2,1)} %all-gather.5.cloned.1.call-done) | copy-start | bytes 6291460
  257.3 490.9 %all-reduce.3.cloned.1.call-start = ((), (), s32[]{:S(2)}) async-start(), calls=%async_computation.6 | async-start | bytes 1048576 | tf_op jit(solution)/shard_map/psum | solution.py:74
  350.3 137.1 %copy-start.4 = (bf16[256,256]{1,0:T(8,128)(2,1)S(1)}, bf16[256,256]{1,0:T(8,128)(2,1)}, u32[]{:S(2)}) copy-start(bf16[256,256]{1,0:T(8,128)(2,1)} %param.10) | copy-start | bytes 393220
Sparse Core Ops, SparseCore 0:
  11.1 100.9 all-gather.2
  127.3 31.7 reduce-scatter.2
  161.5 29.4 all-gather.4
  257.4 227.9 reduce-scatter.4
  491.4 256.7 all-reduce.2
where the time goes:
time: 759 us; the launch traced here: 757 us
  waiting for transfers between devices  551 us (73%)
  blocking collectives  77.5 us (10%)
  other arithmetic  45.9 us (6%)
  local copies, waits for them, and re-layouts  38.4 us (5%)
  matrix products  30.1 us (4%)
  between operations  14.5 us (2%)
    psum x1, waiting for transfers between devices, per_device(): lax.psum((local_msg, local_self, local_bias), ('row', 'col'))  259 us
    reduce_scatter x1, waiting for transfers between devices, per_device(): lax.psum_scatter(back_part.astype(jnp.bfloat16), 'row', scatter_dimension...  130 us
    all_gather x1, waiting for transfers between devices, per_device(): column_msgs = lax.all_gather(messages, 'row', axis=0, tiled=True)  101 us
    psum x1, blocking collectives, per_device(): lax.psum((local_msg, local_self, local_bias), ('row', 'col'))  77.5 us
    reduce_scatter x1, waiting for transfers between devices, per_device(): lax.psum_scatter(partial_value.astype(jnp.bfloat16), 'col', scatter_dimen...  31.9 us
    all_gather x1, waiting for transfers between devices, per_device(): grad_rows_all = lax.all_gather(grad_pre, 'col', axis=0, tiled=True)  29.5 us
    scatter-add x1, other arithmetic, per_device(): jax.ops.segment_sum(backward, slot_cols, num_segments=tile_cols)  28.8 us
  transfers between devices with their start and end apart: 5, of which 5 were waited for; matrix products, arithmetic and copies ran while one was open for 3% of the time, Pallas kernels for 0%

commit v1 on v0

v1 whole, which is shorter than its diff:
```python
import heapq
import math

import jax
import jax.numpy as jnp
from jax import lax
from jax.experimental import pallas as pl
from jax.experimental.pallas import tpu as pltpu
from jax.sharding import PartitionSpec as P

NZ, NY, NX, NC = 8, 4, 4, 8
OWN, FEAT, WIDE, BLK = 512, 256, 128, 128
CAP, TROWS, TCOLS = 96, 32, 128
CUT = 48
HALF = {1: (0, 2), -1: (2, 4)}
ALL = (0, 4)
FIDX, PERM, PROW, SAME, UIDX = 0, 96, 192, 288, 384
TABLE = 512
MESH = pl.DeviceIdType.MESH
BF, F32 = jnp.bfloat16, jnp.float32


def plane_messages():
    out = {}
    low, high = (0, CUT), (CUT, BLK)
    for d in (1, -1):
        out["PY1", d] = ("y", d, (), (0, -d), ALL, low)
        out["QZ", d, 1] = ("z", d, (), (-d, 0), ALL, high)
    for d in (1, -1):
        out["PZ", d, 1, 0] = ("z", d, (), (-d, 0), ALL, low)
        out["QY1", d, 0] = ("y", d, (), (0, -d), ALL, high)
    for d in (1, -1):
        out["PY2", d] = ("y", d, (("PY1", d),), (0, -2 * d), HALF[d], low)
    first = {-1: (("PY1", 1),), 1: (("PY1", -1),), 2: (("PY2", 1), ("PY2", -1))}
    for o in (0, -1, 1, 2):
        for d in (1, -1):
            for t in (1, 2, 3, 4):
                if (o, t) == (0, 1):
                    continue
                parents = first[o] if t == 1 else (("PZ", d, t - 1, o),)
                out["PZ", d, t, o] = ("z", d, parents, (-t * d, o), HALF[d] if t == 4 else ALL, low)
    for d in (1, -1):
        for t in (2, 3, 4):
            blocks = HALF[d] if t == 4 else ALL
            out["QZ", d, t] = ("z", d, (("QZ", d, t - 1),), (-t * d, 0), blocks, high)
    for oz in (0, -1, 1, -2, 2, -3, 3, 4):
        for d in (1, -1):
            if oz == 4:
                parents = (("QZ", 1, 4), ("QZ", -1, 4))
            else:
                parents = (("QZ", 1 if oz < 0 else -1, abs(oz)),)
            if oz:
                out["QY1", d, oz] = ("y", d, parents, (oz, -d), ALL, high)
            out["QY2", d, oz] = ("y", d, (("QY1", d, oz),), (oz, -2 * d), HALF[d], high)
    return out


def rows_in(message):
    (b0, b1), (lo, hi) = message[4:6]
    return (b1 - b0) * (hi - lo)


def plane_order(messages, second):
    rate, latency = 46e3, 1.7
    free, heap, got, order = {}, [], set(), []
    count = 0

    def issue(now, chunk, key):
        nonlocal count
        axis, d = messages[key][:2]
        start = max(now, free.get((axis, d), 0.0))
        free[axis, d] = start + rows_in(messages[key]) * WIDE * 2 / rate
        heapq.heappush(heap, (free[axis, d] + latency, count, chunk, key))
        count += 1

    def roots(now, chunk):
        for key, message in messages.items():
            if not message[2]:
                issue(now, chunk, key)

    roots(0.0, 0)
    heapq.heappush(heap, (second, -1, 1, None))
    while heap:
        now, _, chunk, key = heapq.heappop(heap)
        order.append((chunk, key, now))
        if key is None:
            roots(now, 1)
            continue
        got.add((chunk, key))
        for other, message in messages.items():
            if key in message[2] and all((chunk, p) in got for p in message[2]):
                issue(now, chunk, other)
    return order


MESSAGES = plane_messages()
ORDER = plane_order(MESSAGES, 20.0)
NUMBER = {key: i for i, key in enumerate(MESSAGES)}
COUNT = len(MESSAGES)
OFFSET = {}
_total = 0
for _key, _m in MESSAGES.items():
    OFFSET[_key] = _total
    _total += rows_in(_m)
PLANE_ROWS = _total
CHILDREN = {key: [k for k, m in MESSAGES.items() if key in m[2]] for key in MESSAGES}
ROOTS = [k for k, m in MESSAGES.items() if not m[2]]


def kernel(
    tab, bias, mask, feats, w_msg, w_self, gout, edges,
    hidden, gfeats, edge_out, wgrad, bgrad,
    F0, F1, A, AT, U0, U1, SS0, SS1, SR0, SR1, H0, H1, EB,
    XS0, XS1, XR0, XR1, CS, RX0, RX1, RR0, RR1, SO, SH, GP, GW,
    WC, WR, ZS, ZR, YR, ZG, CG,
    loc, ag_s, ag_r, rs_s, rs_r, x_s, x_r, h_s, h_r, w_s, w_r,
):
    F, U, SS, SR, H = (F0, F1), (U0, U1), (SS0, SS1), (SR0, SR1), (H0, H1)
    XS, XR, RX, RR = (XS0, XS1), (XR0, XR1), (RX0, RX1), (RR0, RR1)
    row = lax.axis_index("row")
    col = lax.axis_index("col")
    z, y = row // NY, row % NY
    x, core = col // 2, col % 2
    other = 1 - core
    sent = []

    def plane_device(dz, dy):
        return ((z + dz) % NZ * NY + (y + dy) % NY, col)

    def col_device(dx, swap=False):
        return (row, (x + dx) % NX * 2 + (other if swap else core))

    def remote(src, dst, ssem, rsem, device):
        return pltpu.make_async_remote_copy(
            src_ref=src, dst_ref=dst, send_sem=ssem, recv_sem=rsem,
            device_id=device, device_id_type=MESH,
        )

    def begin(copy):
        copy.start()
        sent.append(copy)

    def rows_of(start, size, step=16):
        return pl.ds(pl.multiple_of(start, step), size)

    edge_in = pltpu.make_async_copy(edges, A, loc.at[0])
    edge_in.start()
    fm = feats[...] * mask[...].astype(BF)
    for c in (0, 1):
        for n in range(4):
            F[c][row * 4 + n] = fm[n * BLK:(n + 1) * BLK, c * WIDE:(c + 1) * WIDE]
        F[c][TCOLS] = jnp.zeros((BLK, WIDE), BF)
        U[c][CAP] = jnp.zeros((BLK, WIDE), BF)

    barrier = pltpu.get_barrier_semaphore()
    peers = [plane_device(0, d) for d in range(1, NY)]
    peers += [plane_device(d, 0) for d in range(1, NZ)]
    peers += [(row, (col + d) % NC) for d in range(1, NC)]
    for peer in peers:
        pl.semaphore_signal(barrier, inc=1, device_id=peer, device_id_type=MESH)
    pl.semaphore_wait(barrier, len(peers))

    gathers = {}

    def gather_copy(c, key):
        if (c, key) not in gathers:
            axis, d, _, (dz, dy), (b0, b1), (lo, hi) = MESSAGES[key]
            sz, sy = (dz + d, dy) if axis == "z" else (dz, dy + d)
            block = (z + sz) % NZ * NY + (y + sy) % NY
            part = F[c].at[pl.ds(block * 4 + b0, b1 - b0), pl.ds(lo, hi - lo), :]
            i = c * COUNT + NUMBER[key]
            target = plane_device(d, 0) if axis == "z" else plane_device(0, d)
            gathers[c, key] = remote(part, part, ag_s.at[i], ag_r.at[i], target)
        return gathers[c, key]

    def transpose_slot(j):
        def run():
            AT[j] = A[tab[0, PERM + j]].astype(F32).T.astype(BF)
        return run

    def sum_block(c, owner, j, dest, place):
        l = owner * 4 + j
        acc = None
        for k in range(3):
            s = k * TROWS + l
            d = jnp.dot(A[s], F[c][tab[0, FIDX + s]], preferred_element_type=F32)
            acc = d if acc is None else acc + d
        dest[rows_of(place * OWN + j * BLK, BLK, BLK), :] = acc.astype(dest.dtype)

    swaps = {}

    def swap_copy(c, xi):
        if (c, xi) not in swaps:
            part = pl.ds(xi * OWN, OWN)
            swaps[c, xi] = remote(
                XS[c].at[part, :], XR[c].at[part, :],
                x_s.at[c * 8 + xi], x_r.at[c * 8 + xi], col_device(0, True),
            )
        return swaps[c, xi]

    rings = {}
    RING = {("X1", 1): (0, 512), ("X1", -1): (512, 512), ("X2", 1): (1024, 256), ("X2", -1): (1280, 256)}

    def ring_copy(c, key):
        if (c, key) not in rings:
            lo, size = RING[key]
            i = c * 8 + 4 + list(RING).index(key)
            rings[c, key] = remote(
                RX[c].at[pl.ds(lo, size), :], RR[c].at[pl.ds(lo, size), :],
                x_s.at[i], x_r.at[i], col_device(-key[1]),
            )
        return rings[c, key]

    def chip_sum(c, xi, lo, size):
        part = rows_of(xi * OWN + lo, size)
        return CS[part, :] + XR[c][part, :].astype(F32)

    def ring_far(c):
        for xi in range(NX):
            swap_copy(c, xi).wait_recv()
        for d in (1, -1):
            lo, size = RING["X2", d]
            RX[c][pl.ds(lo, size), :] = chip_sum(
                c, (x + 2) % NX, 0 if d > 0 else 256, 256
            ).astype(BF)
            begin(ring_copy(c, ("X2", d)))

    def ring_near(c):
        for d in (1, -1):
            ring_copy(c, ("X2", d)).wait_recv()
            lo = RING["X1", d][0]
            came = RING["X2", d][0]
            to = (x - d) % NX
            for part in (0, 1):
                value = chip_sum(c, to, part * 256, 256)
                if part == (0 if d > 0 else 1):
                    value = value + RR[c][pl.ds(came, 256), :].astype(F32)
                RX[c][pl.ds(lo + part * 256, 256), :] = value.astype(BF)
            begin(ring_copy(c, ("X1", d)))

    def ring_end(c):
        for d in (1, -1):
            ring_copy(c, ("X1", d)).wait_recv()
        SO[:, c * WIDE:(c + 1) * WIDE] = (
            chip_sum(c, x, 0, OWN)
            + RR[c][pl.ds(0, 512), :].astype(F32)
            + RR[c][pl.ds(512, 512), :].astype(F32)
        )

    def sum_slot(c, n):
        def run():
            xi, j = n % 16 // 4, n % 4
            if n < 16:
                sum_block(c, 2 * xi + other, j, XS[c], xi)
                if j == 3:
                    begin(swap_copy(c, xi))
            else:
                sum_block(c, 2 * xi + core, j, CS, xi)
        return run

    for key in ROOTS:
        begin(gather_copy(0, key))
    arrived = set()
    fillers = [edge_in.wait] + [transpose_slot(j) for j in range(CAP)]
    ends = 0
    for chunk, key, _ in ORDER:
        if key is None:
            for root in ROOTS:
                begin(gather_copy(1, root))
            continue
        gather_copy(chunk, key).wait_recv()
        arrived.add((chunk, key))
        for nxt in CHILDREN[key]:
            if all((chunk, p) in arrived for p in MESSAGES[nxt][2]):
                begin(gather_copy(chunk, nxt))
        if chunk == 0 and sum(1 for c, _k in arrived if c == 0) == COUNT:
            fillers += [sum_slot(0, n) for n in range(32)]
            fillers += [None] * 4 + [lambda: ring_far(0)]
            fillers += [None] * 8 + [lambda: ring_near(0)]
        done = 0
        while fillers and done < (1 if ends else 2):
            f = fillers.pop(0)
            done += 1
            if f is not None:
                f()
    for f in fillers:
        if f is not None:
            f()
    ring_end(0)

    @pl.loop(0, 4)
    def _(xi):
        for j in range(4):
            sum_block(1, 2 * xi + other, j, XS[1], xi)

    for xi in range(NX):
        begin(swap_copy(1, xi))

    @pl.loop(0, 4)
    def _(xi):
        for j in range(4):
            sum_block(1, 2 * xi + core, j, CS, xi)

    ring_far(1)
    ring_near(1)
    ring_end(1)

    T_DIM = (((1,), (1,)), ((), ()))
    C_DIM = (((0,), (0,)), ((), ()))

    @pl.loop(0, 4)
    def _(i):
        part = rows_of(i * BLK, BLK, BLK)
        s = SO[part, :]
        hi = s.astype(BF)
        lo = (s - hi.astype(F32)).astype(BF)
        SH[part, :] = hi
        mine = row * 4 + i
        pre = jnp.dot(hi, w_msg[...], preferred_element_type=F32)
        pre += jnp.dot(lo, w_msg[...], preferred_element_type=F32)
        pre += jnp.dot(F0[mine], w_self[:WIDE, :], preferred_element_type=F32)
        pre += jnp.dot(F1[mine], w_self[WIDE:, :], preferred_element_type=F32)
        pre += bias[...]
        real = mask[part, :]
        sig = jax.nn.sigmoid(pre)
        hidden[part, :] = (pre * sig * real).astype(BF)
        deriv = sig * (1.0 + pre * (1.0 - sig))
        gp = (gout[part, :].astype(F32) * real * deriv).astype(BF)
        GP[part, :] = gp
        h = lax.dot_general(gp, w_msg[...], T_DIM, preferred_element_type=F32).astype(BF)
        H0[col * 4 + i] = h[:, :WIDE]
        H1[col * 4 + i] = h[:, WIDE:]

    shares = {}
    SHARE = {
        ("X1", 1): (0, 1, False, -1, 0, 4), ("X1", -1): (1, -1, False, 1, 0, 4),
        ("X2", 1): (2, 1, False, -2, 0, 2), ("X2", -1): (3, -1, False, 2, 2, 2),
        ("S", 0): (4, 0, True, 0, 0, 4), ("S", -1): (5, 0, True, -1, 0, 4),
        ("S", 1): (6, 0, True, 1, 0, 4),
        ("S", 2): (7, 0, True, 2, 0, 2), ("S", 3): (8, 0, True, 2, 2, 2),
    }

    def share_copy(c, key):
        if (c, key) not in shares:
            i, dx, swap, origin, lo, size = SHARE[key]
            from_x = origin if swap else origin + dx
            block = (x + from_x) % NX * 2 + core
            part = H[c].at[pl.ds(block * 4 + lo, size)]
            i += 9 * c
            shares[c, key] = remote(part, part, h_s.at[i], h_r.at[i], col_device(dx, swap))
        return shares[c, key]

    def share_start(c):
        for key in (("X1", 1), ("X1", -1), ("S", 0)):
            begin(share_copy(c, key))

    def share_near(c):
        for d in (1, -1):
            share_copy(c, ("X1", d)).wait_recv()
            begin(share_copy(c, ("X2", d)))
            begin(share_copy(c, ("S", -d)))

    def share_far(c):
        for d in (1, -1):
            share_copy(c, ("X2", d)).wait_recv()
            begin(share_copy(c, ("S", 2 if d > 0 else 3)))

    def share_end(c):
        for n in (0, -1, 1, 2, 3):
            share_copy(c, ("S", n)).wait_recv()

    def term_slots(c, start, count, acc):
        def body(n, acc):
            for u in range(4):
                j = start + n * 4 + u
                h = H[c][tab[0, PROW + j]]
                at = AT[j]
                keep = tab[0, SAME + j].astype(F32)
                acc = acc * keep + jnp.dot(at, h, preferred_element_type=F32)
                U[c][j] = acc.astype(BF)
            return acc
        return lax.fori_loop(0, count // 4, body, acc)

    share_start(0)
    share_start(1)

    WG = WC

    @pl.loop(0, 1)
    def _(i):
        gp = GP[...]
        w1 = lax.dot_general(SH[...], gp, C_DIM, preferred_element_type=F32)
        for n in range(4):
            WG[n, 0:64, :] = w1[n * 64:(n + 1) * 64]
        for c in (0, 1):
            fc = F[c][pl.ds(row * 4, 4)].reshape(OWN, WIDE)
            w2 = lax.dot_general(fc, gp, C_DIM, preferred_element_type=F32)
            for n in range(2):
                WG[4 + 2 * c + n, 0:64, :] = w2[n * 64:(n + 1) * 64]
        b = jnp.sum(gp.astype(F32).reshape(64, 8, FEAT), axis=0)
        for n in range(8):
            WG[n, 64:72, :] = b
        GW[...] = lax.dot_general(gp, w_self[...], T_DIM, preferred_element_type=F32)

    share_near(0)
    share_far(0)
    share_near(1)
    share_end(0)
    zero = jnp.zeros((BLK, WIDE), F32)
    term_slots(0, 0, CAP, zero)

    stages = {}

    def stage_copy(kind, d):
        if (kind, d) not in stages:
            if kind == "col":
                to = (col + d) % NC
                stages[kind, d] = remote(
                    WC.at[to], WR.at[col], w_s.at[d], w_r.at[d], (row, to))
            elif kind == "z":
                to = (z + d) % NZ
                stages[kind, d] = remote(
                    ZS.at[to], ZR.at[z], w_s.at[8 + d], w_r.at[8 + d], plane_device(d, 0))
            elif kind == "y":
                stages[kind, d] = remote(
                    YR.at[y], YR.at[y], w_s.at[16 + d], w_r.at[16 + d], plane_device(0, d))
            elif kind == "zg":
                stages[kind, d] = remote(
                    ZG.at[z], ZG.at[z], w_s.at[20 + d], w_r.at[20 + d], plane_device(d, 0))
            else:
                to = (col + d) % NC
                stages[kind, d] = remote(
                    CG.at[col], CG.at[col], w_s.at[28 + d], w_r.at[28 + d], (row, to))
        return stages[kind, d]

    def stage_send(kind, n):
        for d in range(1, n):
            begin(stage_copy(kind, d))

    def stage_wait(kind, n):
        for d in range(1, n):
            stage_copy(kind, d).wait_recv()

    def weights_0():
        WR[col] = WC[col]
        stage_send("col", NC)

    def weights_1():
        stage_wait("col", NC)
        v = WR[0]
        for n in range(1, NC):
            v = v + WR[n]
        for n in range(NZ):
            ZS[n, 0:8, :] = v[n * 8:n * 8 + 8]
            ZS[n, 8:16, :] = v[64:72]
        ZR[z] = ZS[z]
        stage_send("z", NZ)

    def weights_2():
        stage_wait("z", NZ)
        v = ZR[0]
        for n in range(1, NZ):
            v = v + ZR[n]
        YR[y] = v
        stage_send("y", NY)

    def weights_3():
        stage_wait("y", NY)
        v = (YR[0] + YR[1]) + (YR[2] + YR[3])
        ZG[z] = v[0:8]
        bgrad[...] = v[8:16]
        stage_send("zg", NZ)

    def weights_4():
        stage_wait("zg", NZ)
        for n in range(NZ):
            CG[col, n * 8:n * 8 + 8, :] = ZG[n]
        stage_send("cg", NC)

    def weights_5():
        stage_wait("cg", NC)
        for n in range(NC):
            wgrad[n * 64:(n + 1) * 64, :] = CG[n]

    reduces = {}

    def reduce_copy(c, key):
        if (c, key) not in reduces:
            axis, d = MESSAGES[key][:2]
            part = pl.ds(OFFSET[key], rows_in(MESSAGES[key]))
            i = c * COUNT + NUMBER[key]
            target = plane_device(-d, 0) if axis == "z" else plane_device(0, -d)
            reduces[c, key] = remote(
                SS[c].at[part, :], SR[c].at[part, :], rs_s.at[i], rs_r.at[i], target)
        return reduces[c, key]

    def total_piece(c, block, n, lo, hi, children):
        value = U[c][tab[0, UIDX + block * 4 + n], lo:hi, :].astype(F32)
        for k in children:
            (b0, b1), rows = MESSAGES[k][4:6]
            if rows == (lo, hi) and b0 <= n < b1:
                at = OFFSET[k] + (n - b0) * (hi - lo)
                value = value + SR[c][pl.ds(at, hi - lo), :].astype(F32)
        return value

    waited = set()

    def reduce_wait(c, keys):
        for k in keys:
            if (c, k) not in waited:
                waited.add((c, k))
                reduce_copy(c, k).wait_recv()

    def reduce_send(c, key):
        _, _, _, (dz, dy), (b0, b1), (lo, hi) = MESSAGES[key]
        children = CHILDREN[key]
        reduce_wait(c, children)
        block = (z + dz) % NZ * NY + (y + dy) % NY
        for n in range(b0, b1):
            at = OFFSET[key] + (n - b0) * (hi - lo)
            SS[c][pl.ds(at, hi - lo), :] = total_piece(c, block, n, lo, hi, children).astype(BF)
        begin(reduce_copy(c, key))

    def finish(c):
        reduce_wait(c, ROOTS)
        part = slice(c * WIDE, (c + 1) * WIDE)
        for n in range(4):
            for lo, hi in ((0, CUT), (CUT, BLK)):
                a, b = n * BLK + lo, n * BLK + hi
                value = total_piece(c, row, n, lo, hi, ROOTS) * mask[a:b, :]
                gfeats[a:b, part] = (value + GW[a:b, part]).astype(BF)

    def edge_slot(s):
        def run():
            e = None
            for c in (0, 1):
                f = F[c][tab[0, FIDX + s]]
                d = lax.dot_general(H[c][s % TROWS], f, T_DIM, preferred_element_type=F32)
                e = d if e is None else e + d
            EB[s] = e.astype(BF)
        return run

    plan = [(1 - chunk, key) for chunk, key, _ in reversed(ORDER) if key is not None]
    later = next(i for i, (c, _) in enumerate(plan) if c == 1)
    steps = {16: weights_0, 56: weights_1}
    acc = zero
    edge_work = []
    for i, (c, key) in enumerate(plan):
        if i == later - 12:
            share_far(1)
        if i == later:
            share_end(1)
            term_slots(1, 0, CAP, zero)
            edge_work = [edge_slot(s) for s in range(CAP)]
        reduce_send(c, key)
        if i in steps:
            steps[i]()
        if i > later + 8:
            for _ in range(2):
                if edge_work:
                    edge_work.pop(0)()
        if i == later + 14:
            weights_2()
        if i == later + 26:
            weights_3()
        if i == later + 38:
            weights_4()
        if i == later + 54:
            weights_5()
    for f in edge_work:
        f()
    edge_copy = pltpu.make_async_copy(EB, edge_out, loc.at[1])
    edge_copy.start()
    finish(0)
    finish(1)
    for copy in sent:
        copy.wait_send()
    edge_copy.wait()


def run_kernel(tab, bias, mask, feats, w_msg, w_self, gout, edges):
    vm = pl.BlockSpec(memory_space=pltpu.VMEM)
    dma = pltpu.SemaphoreType.DMA
    b16 = lambda rows: pltpu.VMEM((rows, WIDE), BF)
    f32 = lambda *shape: pltpu.VMEM(shape, F32)
    blocks = lambda n: pltpu.VMEM((n, BLK, WIDE), BF)
    edge_shape = jax.ShapeDtypeStruct((CAP, BLK, BLK), BF)
    scratch = [
        blocks(TCOLS + 1), blocks(TCOLS + 1), blocks(CAP), blocks(CAP),
        blocks(CAP + 1), blocks(CAP + 1),
        b16(PLANE_ROWS), b16(PLANE_ROWS), b16(PLANE_ROWS), b16(PLANE_ROWS),
        blocks(TROWS), blocks(TROWS), blocks(CAP),
        b16(NX * OWN), b16(NX * OWN), b16(NX * OWN), b16(NX * OWN), f32(NX * OWN, WIDE),
        b16(1536), b16(1536), b16(1536), b16(1536),
        f32(OWN, FEAT), pltpu.VMEM((OWN, FEAT), BF), pltpu.VMEM((OWN, FEAT), BF), f32(OWN, FEAT),
        f32(NC, 72, FEAT), f32(NC, 72, FEAT), f32(NZ, 16, FEAT), f32(NZ, 16, FEAT),
        f32(NY, 16, FEAT), f32(NZ, 8, FEAT), f32(NC, 64, FEAT),
        dma((2,)), dma((2 * COUNT,)), dma((2 * COUNT,)), dma((2 * COUNT,)), dma((2 * COUNT,)),
        dma((16,)), dma((16,)), dma((18,)), dma((18,)), dma((36,)), dma((36,)),
    ]
    return pl.pallas_call(
        kernel,
        out_shape=(
            jax.ShapeDtypeStruct((OWN, FEAT), BF),
            jax.ShapeDtypeStruct((OWN, FEAT), BF),
            edge_shape,
            jax.ShapeDtypeStruct((2 * FEAT, FEAT), F32),
            jax.ShapeDtypeStruct((8, FEAT), F32),
        ),
        in_specs=[pl.BlockSpec(memory_space=pltpu.SMEM)] + [vm] * 6
        + [pl.BlockSpec(memory_space=pl.ANY)],
        out_specs=(vm, vm, pl.BlockSpec(memory_space=pl.ANY), vm, vm),
        scratch_shapes=scratch,
        compiler_params=pltpu.CompilerParams(
            collective_id=0, has_side_effects=True, vmem_limit_bytes=64 * 1024 * 1024 - 65536
        ),
    )(tab, bias, mask, feats, w_msg, w_self, gout, edges)


def slot_tables(cols, count):
    s = jnp.arange(CAP, dtype=jnp.int32)
    key = jnp.where(s < count, cols, TCOLS)
    below = (key[None, :] < key[:, None]) | ((key[None, :] == key[:, None]) & (s[None, :] < s[:, None]))
    rank = jnp.sum(below.astype(jnp.int32), axis=1)
    place = (rank[None, :] == s[:, None]).astype(jnp.int32)
    perm = jnp.sum(place * s[None, :], axis=1)
    near = (key[None, :] == key[:, None]) & (s[None, :] < s[:, None])
    again = jnp.any(near, axis=1).astype(jnp.int32)
    same = jnp.sum(place * again[None, :], axis=1)
    m = jnp.arange(TCOLS, dtype=jnp.int32)
    last = jnp.sum((key[None, :] <= m[:, None]).astype(jnp.int32), axis=1) - 1
    has = jnp.any(key[None, :] == m[:, None], axis=1)
    uidx = jnp.where(has, last, CAP)
    return jnp.concatenate([key, perm, perm % TROWS, same, uidx])[None, :]


def per_device(feats, w_msg, w_self, bias, hit_mask, block_cols, block_count, edge_vals, grad_out):
    tab = slot_tables(block_cols[0, 0], block_count[0, 0])
    hidden, gfeats, edge, wgrad, bgrad = run_kernel(
        tab, bias[None, :], hit_mask.astype(F32)[:, None], feats, w_msg, w_self, grad_out,
        edge_vals.reshape(CAP, BLK, BLK),
    )
    factor = 1.0 / math.sqrt(OWN * NZ * NY * NC)
    return (
        hidden,
        gfeats,
        edge.reshape(1, 1, CAP, BLK, BLK),
        wgrad[:FEAT] * factor,
        wgrad[FEAT:] * factor,
        jnp.sum(bgrad, axis=0) * factor,
    )


def solution(mesh):
    placed = (
        P(("row", "col"), None),
        P(),
        P(),
        P(),
        P(("row", "col")),
        P("row", "col", None),
        P("row", "col"),
        P("row", "col", None, None, None),
        P(("row", "col"), None),
    )
    return jax.shard_map(
        per_device,
        mesh=mesh,
        in_specs=placed,
        out_specs=(
            P(("row", "col"), None),
            P(("row", "col"), None),
            P("row", "col", None, None, None),
            P(),
            P(),
            P(),
        ),
        check_vma=False,
    )
```

time: 759 us -> 175 us (0.23)
  waiting for transfers between devices: 551 us -> 0 us
  Pallas kernels: 0 us -> 159 us
  blocking collectives: 77.5 us -> 0 us
  other arithmetic: 45.9 us -> 5.17 us
  matrix products: 30.1 us -> 0 us
  local copies, waits for them, and re-layouts: 38.4 us -> 8.84 us
  between operations: 14.5 us -> 1.32 us
    psum x1 -> x0, waiting for transfers between devices: 259 us -> none  [per_device(): lax.psum((local_msg, local_self, local_bias), ('row', 'col'))]
    reduce_scatter x2 -> x0, waiting for transfers between devices: 162 us -> none  [the longest x1 130 us: per_device(): lax.psum_scatter(back_part.astype(jnp.bfloat16), 'row', scatter_dimension...]
    pallas_call x0 -> x1, Pallas kernels: none -> 159 us  [run_kernel(): pl.pallas_call(kernel, out_shape=(jax.ShapeDtypeStruct((OWN, FEAT), BF),...]
    all_gather x2 -> x0, waiting for transfers between devices: 130 us -> none  [the longest x1 101 us: per_device(): column_msgs = lax.all_gather(messages, 'row', axis=0, tiled=True)]
    psum x1 -> x0, blocking collectives: 77.5 us -> none  [per_device(): lax.psum((local_msg, local_self, local_bias), ('row', 'col'))]
    dot_general x9 -> x0, matrix products: 30.1 us -> none  [the longest x1 7.97 us: per_device(): jnp.einsum('krij,rif->krjf', edge_live, grad_tile, preferred_element_type...]
    scatter-add x1 -> x0, other arithmetic: 28.8 us -> none  [per_device(): jax.ops.segment_sum(backward, slot_cols, num_segments=tile_cols)]
    transpose x2 -> x0, local copies, waits for them, and re-layouts: 19.2 us -> none  [the longest x1 12.6 us: per_device(): jnp.einsum('krij,rif->krjf', edge_live, grad_tile, preferred_element_type...]
  transfers between devices with their start and end apart: 5 -> 0, of which waited for: 5 -> 0; matrix products, arithmetic and copies ran while one was open for 3% -> 0% of each run, Pallas kernels for 0% -> 0%
where the time goes in v1:
time: 175 us
  Pallas kernels  159 us (91%)
  local copies, waits for them, and re-layouts  8.84 us (5%)
  other arithmetic  5.17 us (3%)
    pallas_call x1, Pallas kernels, run_kernel(): pl.pallas_call(kernel, out_shape=(jax.ShapeDtypeStruct((OWN, FEAT), BF),...  159 us
    unnamed x3, local copies, waits for them, and re-layouts  7.3 us

profile of v1, /device:TPU:1, one launch (start us, length us, event | category | flops | bytes accessed | tf_op | source)
XLA Modules:
  0.0 174.6 jit_solution(10764043408316202202)
XLA Ops:
  1.3 0.7 compare_select_fusion.2
  1.9 0.1 convert_reduce_fusion
  2.0 0.1 fusion.1
  2.1 0.2 fusion.2
  2.3 0.2 convert_reduce_fusion.1
  2.5 0.1 select_reduce_fusion
  2.6 0.7 concatenate.3
  3.3 0.7 convert_element_type.20
  4.0 0.9 copy.16.mask
  4.9 159.2 %shard_map.136 = (bf16[512,256]{1,0:T(8,128)(2,1)}, bf16[512,256]{1,0:T(8,128)(2,1)}, bf16[96,128,128]{2,1,0:T(8,128)(2,1)}, f32[512,256]{1,0:T(8,128)}, f32[8,256]{1,0:T(8,128)}) custom-call(s32[1,512]{1,0:T(1,128)} %bitcast.11, f32[1,256]{1,0:T(1,128)} %bitcast.13, f32[512,1]{1,0:T(8,128)} %copy.16.mask, bf16[512,256]{1,0:T(8,128)(2,1)} %feats.1, ...), custom_call_target="tpu_custom_call" | custom-call | tf_op jit(solution)/shard_map/pallas_call | solution.py:601
  164.1 0.7 reduce_sum.49
  164.8 0.6 broadcast_multiply_fusion
  165.4 1.9 %slice_multiply_fusion = (f32[256,256]{1,0:T(8,128)}, f32[256,256]{1,0:T(8,128)}) fusion(f32[512,256]{1,0:T(8,128)} %get-tuple-element.14), kind=kLoop, calls=%fused_computation | loop fusion | flops 131072 | bytes 1048576 | tf_op jit(solution)/shard_map/mul | solution.py:649
  167.3 1.7 copy.21
  168.9 1.7 copy.22
  170.6 4.0 %copy.23 = bf16[1,1,96,128,128]{4,3,2,1,0:T(8,128)(2,1)} copy(bf16[1,1,96,128,128]{4,3,2,1,0:T(8,128)(2,1)} %bitcast.9) | data formatting | bytes 6291456
  (3 shorter events, 0.0 us)

commit v2 on v1

--- a/solution.py
+++ b/solution.py
@@ -17,6 +17,7 @@
 FIDX, PERM, PROW, SAME, UIDX = 0, 96, 192, 288, 384
 TABLE = 512
 MESH = pl.DeviceIdType.MESH
+FACTOR = 1.0 / math.sqrt(OWN * NZ * NY * NC)
 BF, F32 = jnp.bfloat16, jnp.float32
 
 
@@ -60,42 +61,55 @@
     return (b1 - b0) * (hi - lo)
 
 
-def plane_order(messages, second):
-    rate, latency = 46e3, 1.7
-    free, heap, got, order = {}, [], set(), []
-    count = 0
-
-    def issue(now, chunk, key):
-        nonlocal count
-        axis, d = messages[key][:2]
-        start = max(now, free.get((axis, d), 0.0))
-        free[axis, d] = start + rows_in(messages[key]) * WIDE * 2 / rate
-        heapq.heappush(heap, (free[axis, d] + latency, count, chunk, key))
-        count += 1
-
-    def roots(now, chunk):
-        for key, message in messages.items():
-            if not message[2]:
-                issue(now, chunk, key)
-
-    roots(0.0, 0)
-    heapq.heappush(heap, (second, -1, 1, None))
-    while heap:
-        now, _, chunk, key = heapq.heappop(heap)
-        order.append((chunk, key, now))
-        if key is None:
-            roots(now, 1)
-            continue
-        got.add((chunk, key))
-        for other, message in messages.items():
-            if key in message[2] and all((chunk, p) in got for p in message[2]):
-                issue(now, chunk, other)
-    return order
+def plane_order(messages):
+    rate, latency, ahead = 46e3, 1.7, 2.0
+    took = {key: rows_in(m) * WIDE * 2 / rate for key, m in messages.items()}
+    children = {key: [k for k, m in messages.items() if key in m[2]] for key in messages}
+    weight = {}
+
+    def path(key):
+        if key not in weight:
+            weight[key] = took[key] + latency + max([path(k) for k in children[key]] + [0.0])
+        return weight[key]
+
+    links = {m[:2]: 0.0 for m in messages.values()}
+    ready = {link: [] for link in links}
+    got, program, flying = set(), [], []
+
+    def offer(chunk, key):
+        heapq.heappush(ready[messages[key][:2]], (chunk, -path(key), NUMBER[key], key))
+
+    for chunk in (0, 1):
+        for key, m in messages.items():
+            if not m[2]:
+                offer(chunk, key)
+    now = 0.0
+    while True:
+        while flying and flying[0][0] <= now + 1e-9:
+            _, _, chunk, key = heapq.heappop(flying)
+            program.append((False, chunk, key))
+            got.add((chunk, key))
+            for k in children[key]:
+                if all((chunk, p) in got for p in messages[k][2]):
+                    offer(chunk, k)
+        for link in links:
+            while ready[link] and links[link] - ahead <= now + 1e-9:
+                chunk, _, number, key = heapq.heappop(ready[link])
+                links[link] = max(now, links[link]) + took[key]
+                heapq.heappush(flying, (links[link] + latency, len(program), chunk, key))
+                program.append((True, chunk, key))
+        times = [f[0] for f in flying[:1]] + [links[k] - ahead for k in links if ready[k]]
+        if not times:
+            return program, now
+        now = max(now, min(times))
 
 
 MESSAGES = plane_messages()
-ORDER = plane_order(MESSAGES, 20.0)
 NUMBER = {key: i for i, key in enumerate(MESSAGES)}
+PROGRAM, SPAN = plane_order(MESSAGES)
+ORDER = [(chunk, key) for is_send, chunk, key in PROGRAM if not is_send]
+TWIN = {key: (key[0], -key[1]) + key[2:] for key in MESSAGES}
+PAIR = {key: NUMBER[key if key[1] > 0 else TWIN[key]] for key in MESSAGES}
 COUNT = len(MESSAGES)
 OFFSET = {}
 _total = 0
@@ -103,6 +117,7 @@
     OFFSET[_key] = _total
     _total += rows_in(_m)
 PLANE_ROWS = _total
+SLOT = {key: sorted(set(PAIR.values())).index(PAIR[key]) for key in MESSAGES}
 CHILDREN = {key: [k for k, m in MESSAGES.items() if key in m[2]] for key in MESSAGES}
 ROOTS = [k for k, m in MESSAGES.items() if not m[2]]
 
@@ -112,7 +127,7 @@
     hidden, gfeats, edge_out, wgrad, bgrad,
     F0, F1, A, AT, U0, U1, SS0, SS1, SR0, SR1, H0, H1, EB,
     XS0, XS1, XR0, XR1, CS, RX0, RX1, RR0, RR1, SO, SH, GP, GW,
-    WC, WR, ZS, ZR, YR, ZG, CG,
+    WC, WR, ZS, ZR, YR, ZG, CG, ACC,
     loc, ag_s, ag_r, rs_s, rs_r, x_s, x_r, h_s, h_r, w_s, w_r,
 ):
     F, U, SS, SR, H = (F0, F1), (U0, U1), (SS0, SS1), (SR0, SR1), (H0, H1)
@@ -168,10 +183,13 @@
             sz, sy = (dz + d, dy) if axis == "z" else (dz, dy + d)
             block = (z + sz) % NZ * NY + (y + sy) % NY
             part = F[c].at[pl.ds(block * 4 + b0, b1 - b0), pl.ds(lo, hi - lo), :]
-            i = c * COUNT + NUMBER[key]
             target = plane_device(d, 0) if axis == "z" else plane_device(0, d)
-            gathers[c, key] = remote(part, part, ag_s.at[i], ag_r.at[i], target)
+            gathers[c, key] = remote(part, part, ag_s.at[c], ag_r.at[c, SLOT[key]], target)
         return gathers[c, key]
+
+    def pair_wait(c, sem, key):
+        part = SR[c].at[pl.ds(0, 2 * rows_in(MESSAGES[key])), :]
+        pltpu.make_async_copy(part, part, sem.at[c, SLOT[key]]).wait()
 
     def transpose_slot(j):
         def run():
@@ -194,17 +212,20 @@
             part = pl.ds(xi * OWN, OWN)
             swaps[c, xi] = remote(
                 XS[c].at[part, :], XR[c].at[part, :],
-                x_s.at[c * 8 + xi], x_r.at[c * 8 + xi], col_device(0, True),
+                x_s.at[c * 10 + xi], x_r.at[c * 10 + xi], col_device(0, True),
             )
         return swaps[c, xi]
 
     rings = {}
-    RING = {("X1", 1): (0, 512), ("X1", -1): (512, 512), ("X2", 1): (1024, 256), ("X2", -1): (1280, 256)}
+    RING = {
+        ("F", 1): (0, 256), ("F", -1): (256, 256), ("E", 1): (512, 256), ("E", -1): (768, 256),
+        ("L", 1): (1024, 256), ("L", -1): (1280, 256),
+    }
 
     def ring_copy(c, key):
         if (c, key) not in rings:
             lo, size = RING[key]
-            i = c * 8 + 4 + list(RING).index(key)
+            i = c * 10 + 4 + list(RING).index(key)
             rings[c, key] = remote(
                 RX[c].at[pl.ds(lo, size), :], RR[c].at[pl.ds(lo, size), :],
                 x_s.at[i], x_r.at[i], col_device(-key[1]),
@@ -216,36 +237,36 @@
         return CS[part, :] + XR[c][part, :].astype(F32)
 
     def ring_far(c):
-        for xi in range(NX):
-            swap_copy(c, xi).wait_recv()
+        for n in range(4):
+            swap_copy(c, n).wait_recv()
         for d in (1, -1):
-            lo, size = RING["X2", d]
+            lo, size = RING["F", d]
             RX[c][pl.ds(lo, size), :] = chip_sum(
-                c, (x + 2) % NX, 0 if d > 0 else 256, 256
-            ).astype(BF)
-            begin(ring_copy(c, ("X2", d)))
+                c, (x + 2) % NX, 0 if d > 0 else 256, 256).astype(BF)
+            begin(ring_copy(c, ("F", d)))
+        for d in (1, -1):
+            lo, size = RING["E", d]
+            RX[c][pl.ds(lo, size), :] = chip_sum(
+                c, (x - d) % NX, 256 if d > 0 else 0, 256).astype(BF)
+            begin(ring_copy(c, ("E", d)))
 
     def ring_near(c):
         for d in (1, -1):
-            ring_copy(c, ("X2", d)).wait_recv()
-            lo = RING["X1", d][0]
-            came = RING["X2", d][0]
-            to = (x - d) % NX
-            for part in (0, 1):
-                value = chip_sum(c, to, part * 256, 256)
-                if part == (0 if d > 0 else 1):
-                    value = value + RR[c][pl.ds(came, 256), :].astype(F32)
-                RX[c][pl.ds(lo + part * 256, 256), :] = value.astype(BF)
-            begin(ring_copy(c, ("X1", d)))
+            ring_copy(c, ("F", d)).wait_recv()
+            lo, size = RING["L", d]
+            value = chip_sum(c, (x - d) % NX, 0 if d > 0 else 256, 256)
+            value = value + RR[c][pl.ds(RING["F", d][0], 256), :].astype(F32)
+            RX[c][pl.ds(lo, size), :] = value.astype(BF)
+            begin(ring_copy(c, ("L", d)))
 
     def ring_end(c):
-        for d in (1, -1):
-            ring_copy(c, ("X1", d)).wait_recv()
-        SO[:, c * WIDE:(c + 1) * WIDE] = (
-            chip_sum(c, x, 0, OWN)
-            + RR[c][pl.ds(0, 512), :].astype(F32)
-            + RR[c][pl.ds(512, 512), :].astype(F32)
-        )
+        for half in (0, 1):
+            now, old = (("L", 1), ("E", -1)) if half == 0 else (("L", -1), ("E", 1))
+            value = chip_sum(c, x, half * 256, 256)
+            for key in (old, now):
+                ring_copy(c, key).wait_recv()
+                value = value + RR[c][pl.ds(RING[key][0], 256), :].astype(F32)
+            SO[half * 256:(half + 1) * 256, c * WIDE:(c + 1) * WIDE] = value
 
     def sum_slot(c, n):
         def run():
@@ -258,29 +279,24 @@
                 sum_block(c, 2 * xi + core, j, CS, xi)
         return run
 
-    for key in ROOTS:
-        begin(gather_copy(0, key))
     arrived = set()
     fillers = [edge_in.wait] + [transpose_slot(j) for j in range(CAP)]
-    ends = 0
-    for chunk, key, _ in ORDER:
-        if key is None:
-            for root in ROOTS:
-                begin(gather_copy(1, root))
+    left = COUNT
+    for is_send, c, key in PROGRAM:
+        if is_send:
+            gather_copy(c, key).start()
             continue
-        gather_copy(chunk, key).wait_recv()
-        arrived.add((chunk, key))
-        for nxt in CHILDREN[key]:
-            if all((chunk, p) in arrived for p in MESSAGES[nxt][2]):
-                begin(gather_copy(chunk, nxt))
-        if chunk == 0 and sum(1 for c, _k in arrived if c == 0) == COUNT:
-            fillers += [sum_slot(0, n) for n in range(32)]
-            fillers += [None] * 4 + [lambda: ring_far(0)]
-            fillers += [None] * 8 + [lambda: ring_near(0)]
-        done = 0
-        while fillers and done < (1 if ends else 2):
-            f = fillers.pop(0)
-            done += 1
+        if (c, key) not in arrived:
+            arrived |= {(c, key), (c, TWIN[key])}
+            pair_wait(c, ag_r, key)
+        if c == 0:
+            left -= 1
+            if left == 0:
+                fillers += [sum_slot(0, n) for n in range(32)]
+                fillers += [None] * 2 + [lambda: ring_far(0)]
+                fillers += [None] * 5 + [lambda: ring_near(0)]
+        for _ in range(1 if left == 0 else 2):
+            f = fillers.pop(0) if fillers else None
             if f is not None:
                 f()
     for f in fillers:
@@ -288,12 +304,11 @@
             f()
     ring_end(0)
 
-    @pl.loop(0, 4)
-    def _(xi):
-        for j in range(4):
+    for xi in range(NX):
+        @pl.loop(0, 4)
+        def _(j):
             sum_block(1, 2 * xi + other, j, XS[1], xi)
 
-    for xi in range(NX):
         begin(swap_copy(1, xi))
 
     @pl.loop(0, 4)
@@ -382,7 +397,6 @@
         return lax.fori_loop(0, count // 4, body, acc)
 
     share_start(0)
-    share_start(1)
 
     WG = WC
 
@@ -403,8 +417,8 @@
         GW[...] = lax.dot_general(gp, w_self[...], T_DIM, preferred_element_type=F32)
 
     share_near(0)
+    share_start(1)
     share_far(0)
-    share_near(1)
     share_end(0)
     zero = jnp.zeros((BLK, WIDE), F32)
     term_slots(0, 0, CAP, zero)
@@ -468,7 +482,7 @@
         stage_wait("y", NY)
         v = (YR[0] + YR[1]) + (YR[2] + YR[3])
         ZG[z] = v[0:8]
-        bgrad[...] = v[8:16]
+        bgrad[...] = jnp.sum(v[8:16], axis=0, keepdims=True) * FACTOR
         stage_send("zg", NZ)
 
     def weights_4():
@@ -480,7 +494,7 @@
     def weights_5():
         stage_wait("cg", NC)
         for n in range(NC):
-            wgrad[n * 64:(n + 1) * 64, :] = CG[n]
+            wgrad[n * 64:(n + 1) * 64, :] = CG[n] * FACTOR
 
     reduces = {}
 
@@ -488,10 +502,9 @@
         if (c, key) not in reduces:
             axis, d = MESSAGES[key][:2]
             part = pl.ds(OFFSET[key], rows_in(MESSAGES[key]))
-            i = c * COUNT + NUMBER[key]
             target = plane_device(-d, 0) if axis == "z" else plane_device(0, -d)
             reduces[c, key] = remote(
-                SS[c].at[part, :], SR[c].at[part, :], rs_s.at[i], rs_r.at[i], target)
+                SS[c].at[part, :], SR[c].at[part, :], rs_s.at[c], rs_r.at[c, SLOT[key]], target)
         return reduces[c, key]
 
     def total_piece(c, block, n, lo, hi, children):
@@ -509,7 +522,8 @@
         for k in keys:
             if (c, k) not in waited:
                 waited.add((c, k))
-                reduce_copy(c, k).wait_recv()
+                waited.add((c, TWIN[k]))
+                pair_wait(c, rs_r, k)
 
     def reduce_send(c, key):
         _, _, _, (dz, dy), (b0, b1), (lo, hi) = MESSAGES[key]
@@ -519,7 +533,7 @@
         for n in range(b0, b1):
             at = OFFSET[key] + (n - b0) * (hi - lo)
             SS[c][pl.ds(at, hi - lo), :] = total_piece(c, block, n, lo, hi, children).astype(BF)
-        begin(reduce_copy(c, key))
+        reduce_copy(c, key).start()
 
     def finish(c):
         reduce_wait(c, ROOTS)
@@ -540,33 +554,36 @@
             EB[s] = e.astype(BF)
         return run
 
-    plan = [(1 - chunk, key) for chunk, key, _ in reversed(ORDER) if key is not None]
+    plan = [(1 - chunk, key) for chunk, key in reversed(ORDER)]
     later = next(i for i, (c, _) in enumerate(plan) if c == 1)
-    steps = {16: weights_0, 56: weights_1}
-    acc = zero
-    edge_work = []
+
+    def term_filler(n):
+        def run():
+            acc = zero if n == 0 else ACC[...]
+            ACC[...] = term_slots(1, n * 8, 8, acc)
+        return run
+
+    def share_rest():
+        share_far(1)
+        share_end(1)
+
+    edge_work = [lambda: share_near(1), weights_0] + [None] * 10 + [share_rest]
+    edge_work += [term_filler(n) for n in range(CAP // 8)]
+    pace = {later + 6: weights_1, later + 22: weights_2, later + 34: weights_3,
+            later + 46: weights_4, later + 62: weights_5}
     for i, (c, key) in enumerate(plan):
-        if i == later - 12:
-            share_far(1)
         if i == later:
-            share_end(1)
-            term_slots(1, 0, CAP, zero)
+            for f in edge_work:
+                if f is not None:
+                    f()
             edge_work = [edge_slot(s) for s in range(CAP)]
         reduce_send(c, key)
-        if i in steps:
-            steps[i]()
-        if i > later + 8:
-            for _ in range(2):
-                if edge_work:
-                    edge_work.pop(0)()
-        if i == later + 14:
-            weights_2()
-        if i == later + 26:
-            weights_3()
-        if i == later + 38:
-            weights_4()
-        if i == later + 54:
-            weights_5()
+        if i in pace:
+            pace[i]()
+        for _ in range(1 if i < later else 2):
+            f = edge_work.pop(0) if edge_work else None
+            if f is not None:
+                f()
     for f in edge_work:
         f()
     edge_copy = pltpu.make_async_copy(EB, edge_out, loc.at[1])
@@ -575,6 +592,9 @@
     finish(1)
     for copy in sent:
         copy.wait_send()
+    for c in (0, 1):
+        pltpu.make_async_copy(SS[c], SS[c], ag_s.at[c]).wait()
+        pltpu.make_async_copy(SS[c], SS[c], rs_s.at[c]).wait()
     edge_copy.wait()
 
 
@@ -594,9 +614,9 @@
         b16(1536), b16(1536), b16(1536), b16(1536),
         f32(OWN, FEAT), pltpu.VMEM((OWN, FEAT), BF), pltpu.VMEM((OWN, FEAT), BF), f32(OWN, FEAT),
         f32(NC, 72, FEAT), f32(NC, 72, FEAT), f32(NZ, 16, FEAT), f32(NZ, 16, FEAT),
-        f32(NY, 16, FEAT), f32(NZ, 8, FEAT), f32(NC, 64, FEAT),
-        dma((2,)), dma((2 * COUNT,)), dma((2 * COUNT,)), dma((2 * COUNT,)), dma((2 * COUNT,)),
-        dma((16,)), dma((16,)), dma((18,)), dma((18,)), dma((36,)), dma((36,)),
+        f32(NY, 16, FEAT), f32(NZ, 8, FEAT), f32(NC, 64, FEAT), f32(BLK, WIDE),
+        dma((2,)), dma((2,)), dma((2, COUNT // 2)), dma((2,)), dma((2, COUNT // 2)),
+        dma((20,)), dma((20,)), dma((18,)), dma((18,)), dma((36,)), dma((36,)),
     ]
     return pl.pallas_call(
         kernel,
@@ -605,7 +625,7 @@
             jax.ShapeDtypeStruct((OWN, FEAT), BF),
             edge_shape,
             jax.ShapeDtypeStruct((2 * FEAT, FEAT), F32),
-            jax.ShapeDtypeStruct((8, FEAT), F32),
+            jax.ShapeDtypeStruct((1, FEAT), F32),
         ),
         in_specs=[pl.BlockSpec(memory_space=pltpu.SMEM)] + [vm] * 6
         + [pl.BlockSpec(memory_space=pl.ANY)],
@@ -615,6 +635,32 @@
             collective_id=0, has_side_effects=True, vmem_limit_bytes=64 * 1024 * 1024 - 65536
         ),
     )(tab, bias, mask, feats, w_msg, w_self, gout, edges)
+
+
+def hand_over(hidden, gfeats, edge, wgrad, bgrad):
+    def body(h_in, g_in, e_in, w_in, b_in, h, g, e, w1, w2, b, sem):
+        copies = [
+            pltpu.make_async_copy(src, dst, sem.at[i]) for i, (src, dst) in enumerate((
+                (e_in, e), (h_in, h), (g_in, g), (w_in.at[pl.ds(0, FEAT)], w1),
+                (w_in.at[pl.ds(FEAT, FEAT)], w2), (b_in, b),
+            ))
+        ]
+        for copy in copies:
+            copy.start()
+        for copy in copies:
+            copy.wait()
+
+    like = lambda shape, dtype: jax.ShapeDtypeStruct(shape, dtype)
+    return pl.pallas_call(
+        body,
+        out_shape=(
+            like((OWN, FEAT), BF), like((OWN, FEAT), BF), like((CAP, BLK, BLK), BF),
+            like((FEAT, FEAT), F32), like((FEAT, FEAT), F32), like((1, FEAT), F32),
+        ),
+        in_specs=[pl.BlockSpec(memory_space=pltpu.VMEM)] * 5,
+        out_specs=[pl.BlockSpec(memory_space=pl.ANY)] * 6,
+        scratch_shapes=[pltpu.SemaphoreType.DMA((6,))],
+    )(hidden, gfeats, edge, wgrad, bgrad)
 
 
 def slot_tables(cols, count):
@@ -640,15 +686,8 @@
         tab, bias[None, :], hit_mask.astype(F32)[:, None], feats, w_msg, w_self, grad_out,
         edge_vals.reshape(CAP, BLK, BLK),
     )
-    factor = 1.0 / math.sqrt(OWN * NZ * NY * NC)
-    return (
-        hidden,
-        gfeats,
-        edge.reshape(1, 1, CAP, BLK, BLK),
-        wgrad[:FEAT] * factor,
-        wgrad[FEAT:] * factor,
-        jnp.sum(bgrad, axis=0) * factor,
-    )
+    hidden, gfeats, edge, g_msg, g_self, bgrad = hand_over(hidden, gfeats, edge, wgrad, bgrad)
+    return (hidden, gfeats, edge.reshape(1, 1, CAP, BLK, BLK), g_msg, g_self, bgrad[0])
 
 
 def solution(mesh):

time: 175 us -> 164 us (0.937)
  local copies, waits for them, and re-layouts: 8.84 us -> 1.53 us
  other arithmetic: 5.17 us -> 2.02 us
    unnamed x3 -> x0, local copies, waits for them, and re-layouts: 7.3 us -> none
    pallas_call x1, Pallas kernels: 159 us -> 155 us  [run_kernel(): pl.pallas_call(kernel, out_shape=(jax.ShapeDtypeStruct((OWN, FEAT), BF),...]
    pallas_call x0 -> x1, Pallas kernels: none -> 4.28 us  [hand_over(): pl.pallas_call(body, out_shape=(like((OWN, FEAT), BF), like((OWN, FEAT),...]
    mul x2 -> x0, other arithmetic: 2.43 us -> none  [the longest x1 1.86 us: per_device(): wgrad[FEAT:] * factor]
where the time goes in v2:
time: 164 us
  Pallas kernels  159 us (97%)
  other arithmetic  2.02 us (1%)
    pallas_call x1, Pallas kernels, run_kernel(): pl.pallas_call(kernel, out_shape=(jax.ShapeDtypeStruct((OWN, FEAT), BF),...  155 us
    pallas_call x1, Pallas kernels, hand_over(): pl.pallas_call(body, out_shape=(like((OWN, FEAT), BF), like((OWN, FEAT),...  4.28 us

profile of v2, /device:TPU:1, one launch (start us, length us, event | category | flops | bytes accessed | tf_op | source)
XLA Modules:
  0.0 163.8 jit_solution(13606344420971251019)
XLA Ops:
  1.3 0.7 compare_select_fusion.2
  1.9 0.1 convert_reduce_fusion
  2.0 0.1 fusion.1
  2.1 0.2 fusion.2
  2.3 0.2 convert_reduce_fusion.1
  2.5 0.1 select_reduce_fusion
  2.6 0.7 concatenate.3
  3.3 0.7 convert_element_type.20
  4.0 0.9 copy.16.mask
  4.9 154.5 %shard_map.136 = (bf16[512,256]{1,0:T(8,128)(2,1)}, bf16[512,256]{1,0:T(8,128)(2,1)}, bf16[96,128,128]{2,1,0:T(8,128)(2,1)}, f32[512,256]{1,0:T(8,128)}, f32[1,256]{1,0:T(1,128)}) custom-call(s32[1,512]{1,0:T(1,128)} %bitcast.11, f32[1,256]{1,0:T(1,128)} %bitcast.13, f32[512,1]{1,0:T(8,128)} %copy.16.mask, bf16[512,256]{1,0:T(8,128)(2,1)} %feats.1, ...), custom_call_target="tpu_custom_call" | custom-call | tf_op jit(solution)/shard_map/pallas_call | solution.py:621
  159.4 4.3 %shard_map.137 = (bf16[512,256]{1,0:T(8,128)(2,1)}, bf16[512,256]{1,0:T(8,128)(2,1)}, bf16[96,128,128]{2,1,0:T(8,128)(2,1)}, f32[256,256]{1,0:T(8,128)}, f32[256,256]{1,0:T(8,128)}, /*index=5*/f32[1,256]{1,0:T(1,128)}) custom-call(bf16[512,256]{1,0:T(8,128)(2,1)} %get-tuple-element.17.h_in, bf16[512,256]{1,0:T(8,128)(2,1)} %get-tuple-element.18.g_in, ...), custom_call_target="tpu_custom_call" | custom-call | tf_op jit(solution)/shard_map/pallas_call | solution.py:654
  (3 shorter events, 0.0 us)

commit v3 on v2

v3 whole, which is shorter than its diff:
```python
import heapq
import math

import jax
import jax.numpy as jnp
from jax import lax
from jax.experimental import pallas as pl
from jax.experimental.pallas import tpu as pltpu
from jax.sharding import PartitionSpec as P

NZ, NY, NX, NC = 8, 4, 4, 8
OWN, FEAT, WIDE, BLK = 512, 256, 128, 128
CAP, TROWS, TCOLS = 96, 32, 128
CUT = 48
HALF = {1: (0, 2), -1: (2, 4)}
ALL = (0, 4)
NEAR = CAP // 4 * 3
FIDX, PERM, PROW, SAME, UIDX = 0, 96, 192, 288, 384
MESH = pl.DeviceIdType.MESH
FACTOR = 1.0 / math.sqrt(OWN * NZ * NY * NC)
BF, F32 = jnp.bfloat16, jnp.float32


def plane_messages():
    out = {}
    low, high = (0, CUT), (CUT, BLK)
    for d in (1, -1):
        out["PY1", d] = ("y", d, (), (0, -d), ALL, low)
        out["QZ", d, 1] = ("z", d, (), (-d, 0), ALL, high)
    for d in (1, -1):
        out["PZ", d, 1, 0] = ("z", d, (), (-d, 0), ALL, low)
        out["QY1", d, 0] = ("y", d, (), (0, -d), ALL, high)
    for d in (1, -1):
        out["PY2", d] = ("y", d, (("PY1", d),), (0, -2 * d), HALF[d], low)
    first = {-1: (("PY1", 1),), 1: (("PY1", -1),), 2: (("PY2", 1), ("PY2", -1))}
    for o in (0, -1, 1, 2):
        for d in (1, -1):
            for t in (1, 2, 3, 4):
                if (o, t) == (0, 1):
                    continue
                parents = first[o] if t == 1 else (("PZ", d, t - 1, o),)
                out["PZ", d, t, o] = ("z", d, parents, (-t * d, o), HALF[d] if t == 4 else ALL, low)
    for d in (1, -1):
        for t in (2, 3, 4):
            blocks = HALF[d] if t == 4 else ALL
            out["QZ", d, t] = ("z", d, (("QZ", d, t - 1),), (-t * d, 0), blocks, high)
    for oz in (0, -1, 1, -2, 2, -3, 3, 4):
        for d in (1, -1):
            if oz == 4:
                parents = (("QZ", 1, 4), ("QZ", -1, 4))
            else:
                parents = (("QZ", 1 if oz < 0 else -1, abs(oz)),)
            if oz:
                out["QY1", d, oz] = ("y", d, parents, (oz, -d), ALL, high)
            out["QY2", d, oz] = ("y", d, (("QY1", d, oz),), (oz, -2 * d), HALF[d], high)
    return out


def rows_in(message):
    (b0, b1), (lo, hi) = message[4:6]
    return (b1 - b0) * (hi - lo)


RATE, HOP, AHEAD = 46e3, 1.7, 1.5


class Model:
    def __init__(self, messages, back):
        self.messages, self.back = messages, back
        self.took = {key: rows_in(m) * WIDE * 2 / RATE for key, m in messages.items()}
        self.after = {key: [k for k, m in messages.items() if key in m[2]] for key in messages}
        self.links = {m[:2]: 0.0 for m in messages.values()}
        self.landed, self.got, self.flying, self.program = set(), set(), [], []
        self.now, self.weight = 0.0, {}
        self.open, self.waiting = set(), {(c, key) for c in (0, 1) for key in messages}

    def needs(self, key):
        if self.back:
            return self.after[key]
        return self.messages[key][2]

    def path(self, key):
        if key not in self.weight:
            nexts = self.messages[key][2] if self.back else self.after[key]
            self.weight[key] = self.took[key] + HOP + max([self.path(k) for k in nexts] + [0.0])
        return self.weight[key]

    def land(self):
        while self.flying and self.flying[0][0] <= self.now + 1e-9:
            _, _, c, key = heapq.heappop(self.flying)
            self.landed.add((c, key))
            twin = (c, (key[0], -key[1]) + key[2:])
            if twin in self.landed:
                self.got |= {(c, key), twin}
                if not self.back:
                    self.program.append(("recv", c, key))
                    self.now += 0.03

    def send(self):
        best = None
        for c, key in self.waiting:
            link = self.messages[key][:2]
            if c in self.open and self.links[link] - AHEAD <= self.now + 1e-9:
                if all((c, k) in self.got for k in self.needs(key)):
                    rank = (c, -self.path(key), NUMBER[key])
                    if best is None or rank < best[0]:
                        best = (rank, c, key, link)
        if best is None:
            return False
        _, c, key, link = best
        self.waiting.remove((c, key))
        if self.back:
            self.now += 0.05 + self.took[key] * 0.08
        self.links[link] = max(self.now, self.links[link]) + self.took[key]
        heapq.heappush(self.flying, (self.links[link] + HOP, len(self.program), c, key))
        self.program.append(("send", c, key))
        return True

    def run(self, timed, spare):
        last, timed, spare = 0.0, list(timed(self)), list(spare(self))
        while True:
            self.land()
            if self.send():
                continue
            times = [f[0] for f in self.flying[:1]]
            times += [self.links[self.messages[k][:2]] - AHEAD for c, k in self.waiting
                      if c in self.open and all((c, n) in self.got for n in self.needs(k))]
            soon = min([t for t in times if t > self.now] + [1e9])
            if timed and timed[0][3](self) and last + timed[0][2] <= self.now + 1e-9:
                name, cost = timed.pop(0)[:2]
            elif spare and spare[0][2](self) and soon - self.now >= 0.5 * spare[0][1]:
                name, cost = spare.pop(0)[:2]
            else:
                if timed and timed[0][3](self):
                    soon = min(soon, max(last + timed[0][2], self.now + 1e-6))
                if soon > 1e8:
                    return self.program
                self.now = soon
                continue
            self.program.append(("fill",) + name)
            self.now += cost
            if not spare or name[0] not in ("turn", "edge"):
                last = self.now
            if name == ("gate",):
                self.open.add(1)


def gather_program(messages):
    model = Model(messages, False)
    model.open = {0, 1}
    full = lambda m: sum(1 for c, _ in m.got if c == 0) == len(messages)
    timed = [(("sum", n), 0.12, 0.0, full) for n in range(32)]
    timed += [(("far",), 0.2, 1.0, full), (("early",), 0.2, 0.0, full),
              (("near",), 0.2, 3.0, full), (("end",), 0.2, 4.0, full)]
    started = lambda m: m.now > 3.0
    spare = [(("turn", n), 0.12, started) for n in range(CAP + 1)]
    return model.run(lambda m: timed, lambda m: spare), model.now


def reduce_program(messages):
    model = Model(messages, True)
    model.open = {0}
    always = lambda m: True
    timed = [(("share_near",), 0.1, 1.0, always), (("weights", 0), 0.5, 0.0, always),
             (("share_far",), 0.1, 3.5, always), (("share_end",), 0.1, 1.5, always)]
    timed += [(("term", n), 0.4, 0.0, always) for n in range(CAP // 8)] + [(("gate",), 0.0, 0.0, always)]
    timed += [(("weights", n), 0.3, 0.0 if n == 1 else 3.5, always) for n in range(1, 6)]
    opened = lambda m: 1 in m.open
    spare = [(("edge", n), 0.1, opened) for n in range(CAP)]
    return model.run(lambda m: timed, lambda m: spare), model.now


MESSAGES = plane_messages()
NUMBER = {key: i for i, key in enumerate(MESSAGES)}
GATHER, SPAN = gather_program(MESSAGES)
REDUCE, BACK = reduce_program(MESSAGES)
TWIN = {key: (key[0], -key[1]) + key[2:] for key in MESSAGES}
PAIR = {key: NUMBER[key if key[1] > 0 else TWIN[key]] for key in MESSAGES}
COUNT = len(MESSAGES)
OFFSET = {}
_total = 0
for _key, _m in MESSAGES.items():
    OFFSET[_key] = _total
    _total += rows_in(_m)
PLANE_ROWS = _total
SLOT = {key: sorted(set(PAIR.values())).index(PAIR[key]) for key in MESSAGES}
CHILDREN = {key: [k for k, m in MESSAGES.items() if key in m[2]] for key in MESSAGES}
ROOTS = [k for k, m in MESSAGES.items() if not m[2]]


def kernel(
    tab, bias_in, mask_in, feats_in, w_msg_in, w_self_in, gout_in, edges,
    hidden, gfeats, EB, wgrad, bgrad,
    bias, mask, feats, w_msg, w_self, gout, HF0, HF1,
    F0, F1, A, AT, U0, U1, SS0, SS1, SR0, SR1, H0, H1,
    XS0, XS1, XR0, XR1, CS, RX0, RX1, RR0, RR1, SO, SH, GP, GW,
    WC, WR, ZS, ZR, YR, ZG, CG, ACC, MASK,
    loc, ag_s, ag_r, rs_s, rs_r, x_s, x_r, h_s, h_r, w_s, w_r,
):
    F, U, SS, SR, H = (F0, F1), (U0, U1), (SS0, SS1), (SR0, SR1), (H0, H1)
    HF = (HF0, HF1)
    XS, XR, RX, RR = (XS0, XS1), (XR0, XR1), (RX0, RX1), (RR0, RR1)
    row = lax.axis_index("row")
    col = lax.axis_index("col")
    z, y = row // NY, row % NY
    x, core = col // 2, col % 2
    other = 1 - core

    def plane_device(dz, dy):
        return ((z + dz) % NZ * NY + (y + dy) % NY, col)

    def col_device(dx, swap=False):
        return (row, (x + dx) % NX * 2 + (other if swap else core))

    def remote(src, dst, ssem, rsem, device):
        return pltpu.make_async_remote_copy(
            src_ref=src, dst_ref=dst, send_sem=ssem, recv_sem=rsem,
            device_id=device, device_id_type=MESH,
        )

    def rows_of(start, size, step=16):
        return pl.ds(pl.multiple_of(start, step), size)

    edge_in = pltpu.make_async_copy(edges, A, loc.at[0])
    loads = [
        pltpu.make_async_copy(src, dst, loc.at[i + 1])
        for i, (src, dst) in enumerate((
            (feats_in, feats), (mask_in, mask), (w_msg_in, w_msg), (w_self_in, w_self),
            (gout_in, gout), (bias_in, bias),
        ))
    ]
    for load in loads[:2]:
        load.start()
    edge_in.start()
    for load in loads[2:]:
        load.start()
    for load in loads[:2]:
        load.wait()
    flags = mask[...].astype(F32)
    for n in range(4):
        real = jnp.broadcast_to(flags[n:n + 1, :], (BLK, BLK)).T
        MASK[n * BLK:(n + 1) * BLK, :] = real
        for c in (0, 1):
            f = feats[n * BLK:(n + 1) * BLK, c * WIDE:(c + 1) * WIDE]
            F[c][row * 4 + n] = f * real.astype(BF)
    for c in (0, 1):
        F[c][TCOLS] = jnp.zeros((BLK, WIDE), BF)
        U[c][CAP] = jnp.zeros((BLK, WIDE), BF)

    barrier = pltpu.get_barrier_semaphore()
    peers = [plane_device(0, 1), plane_device(0, -1), plane_device(1, 0), plane_device(-1, 0)]
    peers += [col_device(1), col_device(-1), col_device(0, True)]
    for peer in peers:
        pl.semaphore_signal(barrier, inc=1, device_id=peer, device_id_type=MESH)
    pl.semaphore_wait(barrier, len(peers))

    gathers = {}

    def gather_copy(c, key):
        if (c, key) not in gathers:
            axis, d, _, (dz, dy), (b0, b1), (lo, hi) = MESSAGES[key]
            sz, sy = (dz + d, dy) if axis == "z" else (dz, dy + d)
            block = (z + sz) % NZ * NY + (y + sy) % NY
            part = F[c].at[pl.ds(block * 4 + b0, b1 - b0), pl.ds(lo, hi - lo), :]
            target = plane_device(d, 0) if axis == "z" else plane_device(0, d)
            gathers[c, key] = remote(part, part, ag_s.at[c], ag_r.at[c, SLOT[key]], target)
        return gathers[c, key]

    def pair_wait(c, sem, key):
        part = SR[c].at[pl.ds(0, 2 * rows_in(MESSAGES[key])), :]
        pltpu.make_async_copy(part, part, sem.at[c, SLOT[key]]).wait()

    def transpose_slot(j):
        def run():
            AT[j] = A[tab[0, PERM + j]].astype(F32).T.astype(BF)
        return run

    def sum_block(c, owner, j, dest, place):
        l = owner * 4 + j
        acc = None
        for k in range(3):
            s = k * TROWS + l
            d = jnp.dot(A[s], F[c][tab[0, FIDX + s]], preferred_element_type=F32)
            acc = d if acc is None else acc + d
        dest[rows_of(place * OWN + j * BLK, BLK, BLK), :] = acc.astype(dest.dtype)

    swaps = {}

    def swap_copy(c, rel):
        if (c, rel) not in swaps:
            part = rows_of((x + rel) % NX * OWN, OWN)
            swaps[c, rel] = remote(
                XS[c].at[part, :], XR[c].at[part, :], x_s.at[c], x_r.at[c * 10 + rel],
                col_device(0, True),
            )
        return swaps[c, rel]

    rings = {}
    RING = {
        ("F", 1): (0, 256), ("F", -1): (256, 256), ("E", 1): (512, 256), ("E", -1): (768, 256),
        ("L", 1): (1024, 256), ("L", -1): (1280, 256),
    }

    def ring_copy(c, key):
        if (c, key) not in rings:
            lo, size = RING[key]
            i = c * 10 + 4 + list(RING).index(key)
            rings[c, key] = remote(
                RX[c].at[pl.ds(lo, size), :], RR[c].at[pl.ds(lo, size), :],
                x_s.at[2 + c], x_r.at[i], col_device(-key[1]),
            )
        return rings[c, key]

    def chip_sum(c, xi, lo, size):
        part = rows_of(xi * OWN + lo, size)
        return CS[part, :] + XR[c][part, :].astype(F32)

    def ring_far(c):
        swap_copy(c, 2).wait_recv()
        for d in (1, -1):
            lo, size = RING["F", d]
            RX[c][pl.ds(lo, size), :] = chip_sum(
                c, (x + 2) % NX, 0 if d > 0 else 256, 256).astype(BF)
            ring_copy(c, ("F", d)).start()

    def ring_early(c):
        for d in (1, -1):
            swap_copy(c, 3 if d > 0 else 1).wait_recv()
            lo, size = RING["E", d]
            RX[c][pl.ds(lo, size), :] = chip_sum(
                c, (x - d) % NX, 256 if d > 0 else 0, 256).astype(BF)
            ring_copy(c, ("E", d)).start()

    def ring_near(c):
        for d in (1, -1):
            ring_copy(c, ("F", d)).wait_recv()
            lo, size = RING["L", d]
            value = chip_sum(c, (x - d) % NX, 0 if d > 0 else 256, 256)
            value = value + RR[c][pl.ds(RING["F", d][0], 256), :].astype(F32)
            RX[c][pl.ds(lo, size), :] = value.astype(BF)
            ring_copy(c, ("L", d)).start()

    def ring_end(c):
        swap_copy(c, 0).wait_recv()
        for half in (0, 1):
            now, old = (("L", 1), ("E", -1)) if half == 0 else (("L", -1), ("E", 1))
            value = chip_sum(c, x, half * 256, 256)
            for key in (old, now):
                ring_copy(c, key).wait_recv()
                value = value + RR[c][pl.ds(RING[key][0], 256), :].astype(F32)
            SO[half * 256:(half + 1) * 256, c * WIDE:(c + 1) * WIDE] = value

    TURN = (2, 1, 3, 0)

    def sum_slot(c, n):
        rel, j = TURN[n % 16 // 4], n % 4
        xi = (x + rel) % NX
        if n < 16:
            sum_block(c, 2 * xi + other, j, XS[c], xi)
            if j == 3:
                swap_copy(c, rel).start()
        else:
            sum_block(c, 2 * xi + core, j, CS, xi)

    def sum_group(c, rel, mine):
        xi = (x + rel) % NX

        for j in range(4):
            if mine:
                sum_block(c, 2 * xi + core, j, CS, xi)
            else:
                sum_block(c, 2 * xi + other, j, XS[c], xi)

    def turn(n):
        if n == 0:
            edge_in.wait()
            for load in loads[2:]:
                load.wait()
        else:
            transpose_slot(n - 1)()

    gather_steps = {
        "turn": turn, "sum": lambda n: sum_slot(0, n), "far": lambda: ring_far(0),
        "early": lambda: ring_early(0), "near": lambda: ring_near(0), "end": lambda: ring_end(0),
    }
    for step, *what in GATHER:
        if step == "send":
            gather_copy(*what).start()
        elif step == "recv":
            pair_wait(what[0], ag_r, what[1])
        else:
            gather_steps[what[0]](*what[1:])

    for rel in TURN:
        sum_group(1, rel, False)
        swap_copy(1, rel).start()
    sum_group(1, 2, True)
    ring_far(1)
    sum_group(1, 1, True)
    sum_group(1, 3, True)
    ring_early(1)
    sum_group(1, 0, True)
    ring_near(1)
    ring_end(1)

    T_DIM = (((1,), (1,)), ((), ()))
    C_DIM = (((0,), (0,)), ((), ()))

    @pl.loop(0, 4)
    def _(i):
        part = rows_of(i * BLK, BLK, BLK)
        s = SO[part, :]
        hi = s.astype(BF)
        lo = (s - hi.astype(F32)).astype(BF)
        SH[part, :] = hi
        mine = row * 4 + i
        pre = jnp.dot(hi, w_msg[...], preferred_element_type=F32)
        pre += jnp.dot(lo, w_msg[...], preferred_element_type=F32)
        pre += jnp.dot(F0[mine], w_self[:WIDE, :], preferred_element_type=F32)
        pre += jnp.dot(F1[mine], w_self[WIDE:, :], preferred_element_type=F32)
        pre += bias[...]
        real = jnp.concatenate([MASK[part, :], MASK[part, :]], axis=1)
        sig = jax.nn.sigmoid(pre)
        hidden[part, :] = (pre * sig * real).astype(BF)
        deriv = sig * (1.0 + pre * (1.0 - sig))
        gp = (gout[part, :].astype(F32) * real * deriv).astype(BF)
        GP[part, :] = gp
        h = lax.dot_general(gp, w_msg[...], T_DIM, preferred_element_type=F32).astype(BF)
        H0[col * 4 + i] = h[:, :WIDE]
        H1[col * 4 + i] = h[:, WIDE:]

    shares = {}
    SHARE = {
        ("X1", 1): (0, 1, False, -1, 0, 4), ("X1", -1): (1, -1, False, 1, 0, 4),
        ("X2", 1): (2, 1, False, -2, 0, 2), ("X2", -1): (3, -1, False, 2, 2, 2),
        ("S", 0): (4, 0, True, 0, 0, 4), ("S", -1): (5, 0, True, -1, 0, 4),
        ("S", 1): (6, 0, True, 1, 0, 4),
        ("S", 2): (7, 0, True, 2, 0, 2), ("S", 3): (8, 0, True, 2, 2, 2),
    }

    def share_copy(c, key):
        if (c, key) not in shares:
            i, dx, swap, origin, lo, size = SHARE[key]
            from_x = origin if swap else origin + dx
            block = (x + from_x) % NX * 2 + core
            part = H[c].at[pl.ds(block * 4 + lo, size)]
            land = part
            if key[0] == "X2" or lo + size != 4 or key[1] == 3:
                land = HF[c].at[pl.ds(core * 4 + lo, size)]
            if key[0] == "S" and key[1] in (2, 3):
                part = land
            i += 9 * c
            shares[c, key] = remote(part, land, h_s.at[c], h_r.at[i], col_device(dx, swap))
        return shares[c, key]

    def share_start(c):
        for key in (("X1", 1), ("X1", -1), ("S", 0)):
            share_copy(c, key).start()

    def share_near(c):
        for d in (1, -1):
            share_copy(c, ("X1", d)).wait_recv()
            share_copy(c, ("X2", d)).start()
            share_copy(c, ("S", -d)).start()

    def share_far(c):
        for d in (1, -1):
            share_copy(c, ("X2", d)).wait_recv()
            share_copy(c, ("S", 2 if d > 0 else 3)).start()

    def share_end(c, which):
        for n in which:
            share_copy(c, ("S", n)).wait_recv()
        if 3 in which:
            for n in range(8):
                H[c][(x + 2) % NX * 8 + n] = HF[c][n]

    def term_slots(c, start, count, acc, late=False):
        def body(n, acc):
            for u in range(4):
                j = start + n * 4 + u
                h = HF[c][tab[0, PROW + j] & 7] if late else H[c][tab[0, PROW + j]]
                at = AT[j]
                keep = tab[0, SAME + j].astype(F32)
                acc = acc * keep + jnp.dot(at, h, preferred_element_type=F32)
                U[c][j] = acc.astype(BF)
            return acc
        return lax.fori_loop(0, count // 4, body, acc)

    share_start(0)

    WG = WC

    @pl.loop(0, 1)
    def _(i):
        gp = GP[...]
        w1 = lax.dot_general(SH[...], gp, C_DIM, preferred_element_type=F32)
        for n in range(4):
            WG[n, 0:64, :] = w1[n * 64:(n + 1) * 64]
        for c in (0, 1):
            fc = F[c][pl.ds(row * 4, 4)].reshape(OWN, WIDE)
            w2 = lax.dot_general(fc, gp, C_DIM, preferred_element_type=F32)
            for n in range(2):
                WG[4 + 2 * c + n, 0:64, :] = w2[n * 64:(n + 1) * 64]
        b = jnp.sum(gp.astype(F32).reshape(64, 8, FEAT), axis=0)
        for n in range(8):
            WG[n, 64:72, :] = b
        GW[...] = lax.dot_general(gp, w_self[...], T_DIM, preferred_element_type=F32)

    share_near(0)
    share_start(1)
    share_end(0, (0, -1, 1))
    zero = jnp.zeros((BLK, WIDE), F32)
    acc = term_slots(0, 0, 32, zero)
    share_far(0)
    term_slots(0, 32, NEAR - 32, acc)
    share_end(0, (2, 3))
    term_slots(0, NEAR, CAP - NEAR, zero, late=True)

    STAGES = {"col": (0, NC, WR), "z": (1, NZ, ZR), "y": (2, NY, YR), "zg": (3, NZ, ZG), "cg": (4, NC, CG)}

    def stage_send(kind):
        i, n, _ = STAGES[kind]
        for d in range(1, n):
            to_col, to_z = (col + d) % NC, (z + d) % NZ
            src, dst, device = {
                "col": (WC.at[to_col], WR.at[col], (row, to_col)),
                "z": (ZS.at[to_z], ZR.at[z], plane_device(d, 0)),
                "y": (YR.at[y], YR.at[y], plane_device(0, d)),
                "zg": (ZG.at[z], ZG.at[z], plane_device(d, 0)),
                "cg": (CG.at[col], CG.at[col], (row, to_col)),
            }[kind]
            remote(src, dst, w_s.at[i], w_r.at[i], device).start()

    def stage_wait(kind, sems=None):
        i, n, buf = STAGES[kind]
        part = buf.at[pl.ds(0, n - 1)]
        pltpu.make_async_copy(part, part, (w_r if sems is None else sems).at[i]).wait()

    def weights_0():
        WR[col] = WC[col]
        stage_send("col")

    def weights_1():
        stage_wait("col")
        v = WR[0]
        for n in range(1, NC):
            v = v + WR[n]
        for n in range(NZ):
            ZS[n] = jnp.concatenate([v[n * 8:n * 8 + 8], v[64:72]], axis=0).astype(BF)
        ZR[z] = ZS[z]
        stage_send("z")

    def weights_2():
        stage_wait("z")
        v = ZR[0].astype(F32)
        for n in range(1, NZ):
            v = v + ZR[n].astype(F32)
        YR[y] = v.astype(BF)
        stage_send("y")

    def weights_3():
        stage_wait("y")
        v = YR[0].astype(F32)
        for n in range(1, NY):
            v = v + YR[n].astype(F32)
        ZG[z] = v[0:8].astype(BF)
        bgrad[...] = jnp.sum(v[8:16], axis=0, keepdims=True) * FACTOR
        stage_send("zg")

    def weights_4():
        stage_wait("zg")
        for n in range(NZ):
            CG[col, n * 8:n * 8 + 8, :] = ZG[n]
        stage_send("cg")

    def weights_5():
        stage_wait("cg")
        for n in range(NC):
            wgrad[n * 64:(n + 1) * 64, :] = CG[n].astype(F32) * FACTOR

    reduces = {}

    def reduce_copy(c, key):
        if (c, key) not in reduces:
            axis, d = MESSAGES[key][:2]
            part = pl.ds(OFFSET[key], rows_in(MESSAGES[key]))
            target = plane_device(-d, 0) if axis == "z" else plane_device(0, -d)
            reduces[c, key] = remote(
                SS[c].at[part, :], SR[c].at[part, :], rs_s.at[c], rs_r.at[c, SLOT[key]], target)
        return reduces[c, key]

    def total_piece(c, block, n, lo, hi, children):
        m = UIDX + block * 4 + n
        value = U[c][tab[0, m], lo:hi, :].astype(F32) + U[c][tab[0, m + TCOLS], lo:hi, :].astype(F32)
        for k in children:
            (b0, b1), rows = MESSAGES[k][4:6]
            if rows == (lo, hi) and b0 <= n < b1:
                at = OFFSET[k] + (n - b0) * (hi - lo)
                value = value + SR[c][pl.ds(at, hi - lo), :].astype(F32)
        return value

    waited = set()

    def reduce_wait(c, keys):
        for k in keys:
            if (c, k) not in waited:
                waited.add((c, k))
                waited.add((c, TWIN[k]))
                pair_wait(c, rs_r, k)

    def reduce_send(c, key):
        _, _, _, (dz, dy), (b0, b1), (lo, hi) = MESSAGES[key]
        children = CHILDREN[key]
        reduce_wait(c, children)
        block = (z + dz) % NZ * NY + (y + dy) % NY
        for n in range(b0, b1):
            at = OFFSET[key] + (n - b0) * (hi - lo)
            SS[c][pl.ds(at, hi - lo), :] = total_piece(c, block, n, lo, hi, children).astype(BF)
        reduce_copy(c, key).start()

    def finish(c):
        reduce_wait(c, ROOTS)
        part = slice(c * WIDE, (c + 1) * WIDE)
        for n in range(4):
            for lo, hi in ((0, CUT), (CUT, BLK)):
                a, b = n * BLK + lo, n * BLK + hi
                value = total_piece(c, row, n, lo, hi, ROOTS) * MASK[a:b, :]
                gfeats[a:b, part] = (value + GW[a:b, part]).astype(BF)

    def edge_slot(s):
        def run():
            e = None
            for c in (0, 1):
                f = F[c][tab[0, FIDX + s]]
                d = lax.dot_general(H[c][s % TROWS], f, T_DIM, preferred_element_type=F32)
                e = d if e is None else e + d
            EB[s] = e.astype(BF)
        return run

    def term_filler(n):
        acc = zero if n * 8 in (0, NEAR) else ACC[...]
        ACC[...] = term_slots(1, n * 8, 8, acc)

    weights = (weights_0, weights_1, weights_2, weights_3, weights_4, weights_5)
    reduce_steps = {
        "share_near": lambda: share_near(1), "share_far": lambda: share_far(1),
        "share_end": lambda: share_end(1, (0, -1, 1, 2, 3)), "gate": lambda: None,
        "weights": lambda n: weights[n](), "term": term_filler, "edge": lambda n: edge_slot(n)(),
    }
    for step, *what in REDUCE:
        if step == "send":
            reduce_send(*what)
        else:
            reduce_steps[what[0]](*what[1:])
    finish(0)
    finish(1)
    for kind in STAGES:
        stage_wait(kind, w_s)
    for c in (0, 1):
        near = H[c].at[pl.ds(0, 28)]
        pltpu.make_async_copy(near, near, h_s.at[c]).wait()
        pltpu.make_async_copy(XS[c], XS[c], x_s.at[c]).wait()
        pltpu.make_async_copy(RX[c], RX[c], x_s.at[2 + c]).wait()
        pltpu.make_async_copy(SS[c], SS[c], ag_s.at[c]).wait()
        pltpu.make_async_copy(SS[c], SS[c], rs_s.at[c]).wait()


def run_kernel(tab, bias, mask, feats, w_msg, w_self, gout, edges):
    vm = pl.BlockSpec(memory_space=pltpu.VMEM)
    dma = pltpu.SemaphoreType.DMA
    b16 = lambda rows: pltpu.VMEM((rows, WIDE), BF)
    f32 = lambda *shape: pltpu.VMEM(shape, F32)
    half = lambda *shape: pltpu.VMEM(shape, BF)
    blocks = lambda n: pltpu.VMEM((n, BLK, WIDE), BF)
    edge_shape = jax.ShapeDtypeStruct((CAP, BLK, BLK), BF)
    scratch = [
        f32(1, FEAT), pltpu.VMEM((4, BLK), jnp.int32), pltpu.VMEM((OWN, FEAT), BF),
        pltpu.VMEM((FEAT, FEAT), BF), pltpu.VMEM((FEAT, FEAT), BF), pltpu.VMEM((OWN, FEAT), BF),
        pltpu.VMEM((8, BLK, WIDE), BF), pltpu.VMEM((8, BLK, WIDE), BF),
        blocks(TCOLS + 1), blocks(TCOLS + 1), blocks(CAP), blocks(CAP),
        blocks(CAP + 1), blocks(CAP + 1),
        b16(PLANE_ROWS), b16(PLANE_ROWS), b16(PLANE_ROWS), b16(PLANE_ROWS),
        blocks(TROWS), blocks(TROWS),
        b16(NX * OWN), b16(NX * OWN), b16(NX * OWN), b16(NX * OWN), f32(NX * OWN, WIDE),
        b16(1536), b16(1536), b16(1536), b16(1536),
        f32(OWN, FEAT), pltpu.VMEM((OWN, FEAT), BF), pltpu.VMEM((OWN, FEAT), BF), f32(OWN, FEAT),
        f32(NC, 72, FEAT), f32(NC, 72, FEAT), half(NZ, 16, FEAT), half(NZ, 16, FEAT),
        half(NY, 16, FEAT), half(NZ, 8, FEAT), half(NC, 64, FEAT), f32(BLK, WIDE), f32(OWN, WIDE),
        dma((7,)), dma((2,)), dma((2, COUNT // 2)), dma((2,)), dma((2, COUNT // 2)),
        dma((4,)), dma((20,)), dma((2,)), dma((18,)), dma((5,)), dma((5,)),
    ]
    return pl.pallas_call(
        kernel,
        out_shape=(
            jax.ShapeDtypeStruct((OWN, FEAT), BF),
            jax.ShapeDtypeStruct((OWN, FEAT), BF),
            edge_shape,
            jax.ShapeDtypeStruct((2 * FEAT, FEAT), F32),
            jax.ShapeDtypeStruct((1, FEAT), F32),
        ),
        in_specs=[pl.BlockSpec(memory_space=pltpu.SMEM)]
        + [pl.BlockSpec(memory_space=pltpu.HBM)] * 7,
        out_specs=(vm,) * 5,
        scratch_shapes=scratch,
        compiler_params=pltpu.CompilerParams(
            collective_id=0, has_side_effects=True, vmem_limit_bytes=48 * 1024 * 1024
        ),
    )(tab, *[pltpu.with_memory_space_constraint(v, pltpu.HBM)
             for v in (bias, mask, feats, w_msg, w_self, gout, edges)])


def hand_over(hidden, gfeats, edge, wgrad, bgrad):
    def body(h_in, g_in, e_in, w_in, b_in, h, g, e, w1, w2, b, sem):
        copies = [
            pltpu.make_async_copy(src, dst, sem.at[i]) for i, (src, dst) in enumerate((
                (e_in, e), (h_in, h), (g_in, g), (w_in.at[pl.ds(0, FEAT)], w1),
                (w_in.at[pl.ds(FEAT, FEAT)], w2), (b_in, b),
            ))
        ]
        for copy in copies:
            copy.start()
        for copy in copies:
            copy.wait()

    like = lambda shape, dtype: jax.ShapeDtypeStruct(shape, dtype)
    return pl.pallas_call(
        body,
        out_shape=(
            like((OWN, FEAT), BF), like((OWN, FEAT), BF), like((CAP, BLK, BLK), BF),
            like((FEAT, FEAT), F32), like((FEAT, FEAT), F32), like((1, FEAT), F32),
        ),
        in_specs=[pl.BlockSpec(memory_space=pltpu.VMEM)] * 5,
        out_specs=[pl.BlockSpec(memory_space=pl.ANY)] * 6,
        scratch_shapes=[pltpu.SemaphoreType.DMA((6,))],
        compiler_params=pltpu.CompilerParams(vmem_limit_bytes=8 * 1024 * 1024),
    )(hidden, gfeats, edge, wgrad, bgrad)


def slot_tables(cols, count, far):
    s = jnp.arange(CAP, dtype=jnp.int32)
    key = jnp.where(s < count, cols, TCOLS)
    late = s % TROWS // 8 == far
    order = key + jnp.where(late, TCOLS + 1, 0)
    before = (order[None, :] == order[:, None]) & (s[None, :] < s[:, None])
    rank = jnp.sum(((order[None, :] < order[:, None]) | before).astype(jnp.int32), axis=1)
    again = jnp.any(before, axis=1).astype(jnp.int32)
    place = (rank[None, :] == s[:, None]).astype(jnp.int32)
    perm = jnp.sum(place * s[None, :], axis=1)
    same = jnp.sum(place * again[None, :], axis=1)
    m = jnp.arange(2 * TCOLS, dtype=jnp.int32)
    want = m + jnp.where(m < TCOLS, 0, 1)
    last = jnp.max(jnp.where(order[None, :] == want[:, None], rank[None, :], -1), axis=1)
    uidx = jnp.where(last < 0, CAP, last)
    return jnp.concatenate([key, perm, perm % TROWS, same, uidx])[None, :]


def per_device(feats, w_msg, w_self, bias, hit_mask, block_cols, block_count, edge_vals, grad_out):
    far = (lax.axis_index("col") // 2 + 2) % NX
    tab = slot_tables(block_cols[0, 0], block_count[0, 0], far)
    hidden, gfeats, edge, wgrad, bgrad = run_kernel(
        tab, bias[None, :], hit_mask.reshape(4, BLK), feats, w_msg, w_self, grad_out,
        edge_vals.reshape(CAP, BLK, BLK),
    )
    hidden, gfeats, edge, g_msg, g_self, bgrad = hand_over(hidden, gfeats, edge, wgrad, bgrad)
    return (hidden, gfeats, edge.reshape(1, 1, CAP, BLK, BLK), g_msg, g_self, bgrad[0])


def solution(mesh):
    placed = (
        P(("row", "col"), None),
        P(),
        P(),
        P(),
        P(("row", "col")),
        P("row", "col", None),
        P("row", "col"),
        P("row", "col", None, None, None),
        P(("row", "col"), None),
    )
    return jax.shard_map(
        per_device,
        mesh=mesh,
        in_specs=placed,
        out_specs=(
            P(("row", "col"), None),
            P(("row", "col"), None),
            P("row", "col", None, None, None),
            P(),
            P(),
            P(),
        ),
        check_vma=False,
    )
```

time: 164 us -> 142 us (0.87)
  Pallas kernels: 159 us -> 139 us
    pallas_call x1, Pallas kernels: 155 us -> 137 us  [run_kernel(): pl.pallas_call(kernel, out_shape=(jax.ShapeDtypeStruct((OWN, FEAT), BF),...]
    pallas_call x1, Pallas kernels: 4.28 us -> 2.05 us  [hand_over(): pl.pallas_call(body, out_shape=(like((OWN, FEAT), BF), like((OWN, FEAT),...]
where the time goes in v3:
time: 142 us
  Pallas kernels  139 us (98%)
  between operations  1.52 us (1%)
    pallas_call x1, Pallas kernels, run_kernel(): pl.pallas_call(kernel, out_shape=(jax.ShapeDtypeStruct((OWN, FEAT), BF),...  137 us

profile of v3, /device:TPU:1, one launch (start us, length us, event | category | flops | bytes accessed | tf_op | source)
XLA Modules:
  0.0 142.3 jit_solution(17254180539834839922)
XLA Ops:
  1.3 0.7 fusion.3
  2.0 0.2 convert_reduce_fusion
  2.1 0.2 fusion.1
  2.3 0.1 select_reduce_fusion.1
  2.5 0.1 select_reduce_fusion
  2.6 0.1 concatenate.3
  2.7 137.4 %shard_map.136 = (bf16[512,256]{1,0:T(8,128)(2,1)S(1)}, bf16[512,256]{1,0:T(8,128)(2,1)S(1)}, bf16[96,128,128]{2,1,0:T(8,128)(2,1)S(1)}, f32[512,256]{1,0:T(8,128)S(1)}, f32[1,256]{1,0:T(1,128)S(1)}) custom-call(s32[1,640]{1,0:T(1,128)S(1)} %broadcast_in_dim.60.tab, f32[1,256]{1,0:T(1,128)} %bitcast.12, s32[4,128]{1,0:T(4,128)} %bitcast.11, ...), custom_call_target="tpu_custom_call" | custom-call | tf_op jit(solution)/shard_map/pallas_call | solution.py:693
  140.1 2.1 %shard_map.137 = (bf16[512,256]{1,0:T(8,128)(2,1)}, bf16[512,256]{1,0:T(8,128)(2,1)}, bf16[96,128,128]{2,1,0:T(8,128)(2,1)}, f32[256,256]{1,0:T(8,128)}, f32[256,256]{1,0:T(8,128)}, /*index=5*/f32[1,256]{1,0:T(1,128)}) custom-call(bf16[512,256]{1,0:T(8,128)(2,1)S(1)} %get-tuple-element.17.h_in, bf16[512,256]{1,0:T(8,128)(2,1)S(1)} %get-tuple-element.18.g_in, ...), custom_call_target="tpu_custom_call" | custom-call | tf_op jit(solution)/shard_map/pallas_call | solution.py:727
  (5 shorter events, 0.0 us)

commit v4 on v3

--- a/solution.py
+++ b/solution.py
@@ -61,12 +61,14 @@
     return (b1 - b0) * (hi - lo)
 
 
-RATE, HOP, AHEAD = 46e3, 1.7, 1.5
+RATE, HOP = 46e3, 1.7
+GATHER_AHEAD, REDUCE_AHEAD = 1.5, 1.5
 
 
 class Model:
     def __init__(self, messages, back):
         self.messages, self.back = messages, back
+        self.ahead = REDUCE_AHEAD if back else GATHER_AHEAD
         self.took = {key: rows_in(m) * WIDE * 2 / RATE for key, m in messages.items()}
         self.after = {key: [k for k, m in messages.items() if key in m[2]] for key in messages}
         self.links = {m[:2]: 0.0 for m in messages.values()}
@@ -100,7 +102,7 @@
         best = None
         for c, key in self.waiting:
             link = self.messages[key][:2]
-            if c in self.open and self.links[link] - AHEAD <= self.now + 1e-9:
+            if c in self.open and self.links[link] - self.ahead <= self.now + 1e-9:
                 if all((c, k) in self.got for k in self.needs(key)):
                     rank = (c, -self.path(key), NUMBER[key])
                     if best is None or rank < best[0]:
@@ -123,7 +125,7 @@
             if self.send():
                 continue
             times = [f[0] for f in self.flying[:1]]
-            times += [self.links[self.messages[k][:2]] - AHEAD for c, k in self.waiting
+            times += [self.links[self.messages[k][:2]] - self.ahead for c, k in self.waiting
                       if c in self.open and all((c, n) in self.got for n in self.needs(k))]
             soon = min([t for t in times if t > self.now] + [1e9])
             if timed and timed[0][3](self) and last + timed[0][2] <= self.now + 1e-9:
@@ -234,6 +236,11 @@
     edge_in.start()
     for load in loads[2:]:
         load.start()
+    barrier = pltpu.get_barrier_semaphore()
+    peers = [plane_device(0, 1), plane_device(0, -1), plane_device(1, 0), plane_device(-1, 0)]
+    peers += [col_device(1), col_device(-1), col_device(0, True)]
+    for peer in peers:
+        pl.semaphore_signal(barrier, inc=1, device_id=peer, device_id_type=MESH)
     for load in loads[:2]:
         load.wait()
     flags = mask[...].astype(F32)
@@ -247,11 +254,6 @@
         F[c][TCOLS] = jnp.zeros((BLK, WIDE), BF)
         U[c][CAP] = jnp.zeros((BLK, WIDE), BF)
 
-    barrier = pltpu.get_barrier_semaphore()
-    peers = [plane_device(0, 1), plane_device(0, -1), plane_device(1, 0), plane_device(-1, 0)]
-    peers += [col_device(1), col_device(-1), col_device(0, True)]
-    for peer in peers:
-        pl.semaphore_signal(barrier, inc=1, device_id=peer, device_id_type=MESH)
     pl.semaphore_wait(barrier, len(peers))
 
     gathers = {}
@@ -406,9 +408,8 @@
     T_DIM = (((1,), (1,)), ((), ()))
     C_DIM = (((0,), (0,)), ((), ()))
 
-    @pl.loop(0, 4)
-    def _(i):
-        part = rows_of(i * BLK, BLK, BLK)
+    for i in range(4):
+        part = pl.ds(i * BLK, BLK)
         s = SO[part, :]
         hi = s.astype(BF)
         lo = (s - hi.astype(F32)).astype(BF)
@@ -475,17 +476,17 @@
             for n in range(8):
                 H[c][(x + 2) % NX * 8 + n] = HF[c][n]
 
-    def term_slots(c, start, count, acc, late=False):
+    def term_slots(c, start, count, acc, late=False, size=12):
         def body(n, acc):
-            for u in range(4):
-                j = start + n * 4 + u
+            for u in range(size):
+                j = start + n * size + u
                 h = HF[c][tab[0, PROW + j] & 7] if late else H[c][tab[0, PROW + j]]
                 at = AT[j]
                 keep = tab[0, SAME + j].astype(F32)
                 acc = acc * keep + jnp.dot(at, h, preferred_element_type=F32)
                 U[c][j] = acc.astype(BF)
             return acc
-        return lax.fori_loop(0, count // 4, body, acc)
+        return body(0, acc) if count == size else lax.fori_loop(0, count // size, body, acc)
 
     share_start(0)
 
@@ -511,9 +512,9 @@
     share_start(1)
     share_end(0, (0, -1, 1))
     zero = jnp.zeros((BLK, WIDE), F32)
-    acc = term_slots(0, 0, 32, zero)
+    acc = term_slots(0, 0, 36, zero)
     share_far(0)
-    term_slots(0, 32, NEAR - 32, acc)
+    term_slots(0, 36, NEAR - 36, acc)
     share_end(0, (2, 3))
     term_slots(0, NEAR, CAP - NEAR, zero, late=True)
 
@@ -640,7 +641,7 @@
 
     def term_filler(n):
         acc = zero if n * 8 in (0, NEAR) else ACC[...]
-        ACC[...] = term_slots(1, n * 8, 8, acc)
+        ACC[...] = term_slots(1, n * 8, 8, acc, size=8)
 
     weights = (weights_0, weights_1, weights_2, weights_3, weights_4, weights_5)
     reduce_steps = {

time: 142 us -> 140 us (0.986)
  Pallas kernels: 139 us -> 137 us
    pallas_call x1, Pallas kernels: 137 us -> 135 us  [run_kernel(): pl.pallas_call(kernel, out_shape=(jax.ShapeDtypeStruct((OWN, FEAT), BF),...]
where the time goes in v4:
time: 140 us; the launch traced here: 139 us
  Pallas kernels  137 us (98%)
  between operations  1.52 us (1%)
    pallas_call x1, Pallas kernels, run_kernel(): pl.pallas_call(kernel, out_shape=(jax.ShapeDtypeStruct((OWN, FEAT), BF),...  135 us

profile of v4, /device:TPU:1, one launch (start us, length us, event | category | flops | bytes accessed | tf_op | source)
XLA Modules:
  0.0 139.5 jit_solution(3112976895278206997)
XLA Ops:
  1.3 0.7 fusion.3
  2.0 0.2 convert_reduce_fusion
  2.1 0.2 fusion.1
  2.3 0.1 select_reduce_fusion.1
  2.5 0.1 select_reduce_fusion
  2.6 0.1 concatenate.3
  2.7 134.6 %shard_map.136 = (bf16[512,256]{1,0:T(8,128)(2,1)S(1)}, bf16[512,256]{1,0:T(8,128)(2,1)S(1)}, bf16[96,128,128]{2,1,0:T(8,128)(2,1)S(1)}, f32[512,256]{1,0:T(8,128)S(1)}, f32[1,256]{1,0:T(1,128)S(1)}) custom-call(s32[1,640]{1,0:T(1,128)S(1)} %broadcast_in_dim.60.tab, f32[1,256]{1,0:T(1,128)} %bitcast.12, s32[4,128]{1,0:T(4,128)} %bitcast.11, ...), custom_call_target="tpu_custom_call" | custom-call | tf_op jit(solution)/shard_map/pallas_call | solution.py:694
  137.3 2.1 %shard_map.137 = (bf16[512,256]{1,0:T(8,128)(2,1)}, bf16[512,256]{1,0:T(8,128)(2,1)}, bf16[96,128,128]{2,1,0:T(8,128)(2,1)}, f32[256,256]{1,0:T(8,128)}, f32[256,256]{1,0:T(8,128)}, /*index=5*/f32[1,256]{1,0:T(1,128)}) custom-call(bf16[512,256]{1,0:T(8,128)(2,1)S(1)} %get-tuple-element.17.h_in, bf16[512,256]{1,0:T(8,128)(2,1)S(1)} %get-tuple-element.18.g_in, ...), custom_call_target="tpu_custom_call" | custom-call | tf_op jit(solution)/shard_map/pallas_call | solution.py:728
  (5 shorter events, 0.0 us)
